TPU v7x, 512 devices: a whole 4x4x16 slice. The times are simulated.
512 devices in a mesh: samp: 128 (over z, y, core), cell: 4 (over x).
Axes of the slice: x: 4, y: 4, z: 16, core: 2. Of those that a mesh axis runs over, the one named last changes fastest.
Arguments:
- points: float32 [24, 262144], P(None, 'samp'), may hold values from -1 to 1
- yields: bfloat16 [262144, 1024], P('samp', 'cell'), may hold values from -6 to 6
- term_index: int32 [512, 2], replicated, may hold values from 0 to 95, as said below
- block_group: int32 [8], replicated, may hold values from 0 to 7
Outputs:
- coefficients: float32 [512, 1024], P('cell')
- sobol: float32 [8, 1024], P(None, 'cell')
Inputs may be any that keep to these rules, and one draw needn't show every extreme that they name: `term_index`: row 0 is 0, 0 (the constant term); every other row names one parameter with degree 1 to 3 and column 0, or two different parameters with degrees 1 to 3 each, the lower column first; no two rows are the same.
All inputs are finite; a program needn't handle non-finite values.
Results may differ from a plain program's by a relative error of at most 0.0037.
Values sent between devices are 32-bit elements; how exact they have to be, the bound alone decides.
A program may use at most 64 MiB of HBM per device.

v0:
```python
import jax
import jax.numpy as jnp
from jax import lax
from jax.sharding import PartitionSpec as P

BLOCK = 64
GROUPS = 8


def basis_rows(xs):
    ones = jnp.ones_like(xs)
    first = 1.7320508075688772 * xs
    second = 2.23606797749979 * (1.5 * xs * xs - 0.5)
    third = 2.6457513110645907 * (2.5 * xs * xs * xs - 1.5 * xs)
    stacked = jnp.stack([ones, first, second, third], axis=1)
    return stacked.reshape(4 * xs.shape[0], xs.shape[1])


def design(xs, term_index):
    table = basis_rows(xs)
    left = jnp.take(table, term_index[:, 0], axis=0)
    right = jnp.take(table, term_index[:, 1], axis=0)
    return (left * right).astype(jnp.bfloat16)


def on_device(points, yields, term_index, block_group):
    psi = design(points, term_index)
    cross_local = jnp.dot(psi, yields, preferred_element_type=jnp.float32)
    gram_local = jnp.dot(psi, psi.T, preferred_element_type=jnp.float32)
    gram, cross = lax.psum((gram_local, cross_local), "samp")
    lower = jnp.linalg.cholesky(gram)
    inner = lax.linalg.triangular_solve(lower, cross, left_side=True, lower=True)
    coef = lax.linalg.triangular_solve(lower, inner, left_side=True, lower=True, transpose_a=True)
    total_samples = points.shape[1] * lax.axis_size("samp")
    scaled = coef * jnp.sqrt(jnp.float32(total_samples))
    terms = coef.shape[0]
    keep = (jnp.arange(terms) >= 1).astype(jnp.float32)
    squares = coef * coef * keep[:, None]
    groups = jnp.repeat(block_group, BLOCK)
    member = (groups[None, :] == jnp.arange(GROUPS, dtype=jnp.int32)[:, None]).astype(jnp.float32)
    part = jnp.dot(member, squares, precision=lax.Precision.HIGHEST)
    total = jnp.sum(squares, axis=0)
    sobol = part / total[None, :]
    coefficients = lax.all_to_all(scaled, "cell", split_axis=0, concat_axis=1, tiled=True)
    return (coefficients, sobol)


def solution(mesh):
    placed = (P(None, "samp"), P("samp", "cell"), P(), P())
    return jax.shard_map(
        on_device,
        mesh=mesh,
        in_specs=placed,
        out_specs=(P("cell", None), P(None, "cell")),
        check_vma=False,
    )
```

profile of v0, /device:TPU:1, one launch (start us, length us, event | category | flops | bytes accessed | tf_op | source)
XLA Modules:
  0.0 540.1 jit_solution(15287291031429529462)
XLA Ops:
  7.2 0.8 fusion.59
  8.0 1.0 multiply_bitcast_fusion
  10.0 3.6 gather_fusion
  13.6 3.6 gather_fusion.1
  17.2 4.0 fusion
  21.2 2.3 fusion.60
  23.6 1.5 fusion.61
  25.1 349.1 %all-reduce.4.cloned.1.call-done = (f32[512,256]{1,0:T(8,128)}, f32[512,512]{0,1:T(8,128)}) async-done(((f32[512,256]{1,0:T(8,128)}, f32[512,512]{0,1:T(8,128)}), (f32[512,256]{1,0:T(8,128)}, f32[512,512]{0,1:T(8,128)})) %all-reduce.4.cloned.1.call-update) | async-done | bytes 1572880 | tf_op jit(solution)/shard_map/psum | solution.py:30
  374.2 1.6 copy.8
  375.8 1.5 fusion.1
  377.2 11.7 %cholesky.104 = f32[128,128]{1,0:T(8,128)S(1)} custom-call(f32[128,128]{1,0:T(8,128)S(1)} %cholesky.266), custom_call_target="Cholesky" | custom-call | tf_op jit(solution)/shard_map/jit(cholesky)/cholesky | solution.py:31
  389.1 9.8 %custom-call.32 = f32[1,128,128]{1,2,0:T(8,128)S(1)} custom-call(f32[1,128,128]{2,1,0:T(8,128)S(1)} %get-tuple-element.37), custom_call_target="InvertDiagBlocksLowerTriangular" | custom-call | tf_op jit(solution)/shard_map/jit(cholesky)/cholesky | solution.py:31
  399.6 11.9 %cholesky.217 = f32[128,128]{1,0:T(8,128)S(1)} custom-call(f32[128,128]{1,0:T(8,128)S(1)} %cholesky.270), custom_call_target="Cholesky" | custom-call | tf_op jit(solution)/shard_map/jit(cholesky)/cholesky | solution.py:31
  412.9 9.8 %custom-call.33 = f32[1,128,128]{1,2,0:T(8,128)S(1)} custom-call(f32[1,128,128]{2,1,0:T(8,128)S(1)} %get-tuple-element.34), custom_call_target="InvertDiagBlocksLowerTriangular" | custom-call | tf_op jit(solution)/shard_map/jit(cholesky)/cholesky | solution.py:31
  423.4 11.7 %cholesky.238 = f32[128,128]{1,0:T(8,128)S(1)} custom-call(f32[128,128]{1,0:T(8,128)S(1)} %cholesky.275), custom_call_target="Cholesky" | custom-call | tf_op jit(solution)/shard_map/jit(cholesky)/cholesky | solution.py:31
  435.8 9.8 %custom-call.34 = f32[1,128,128]{1,2,0:T(8,128)S(1)} custom-call(f32[1,128,128]{2,1,0:T(8,128)S(1)} %get-tuple-element.31), custom_call_target="InvertDiagBlocksLowerTriangular" | custom-call | tf_op jit(solution)/shard_map/jit(cholesky)/cholesky | solution.py:31
  446.2 11.9 %cholesky.255 = f32[128,128]{1,0:T(8,128)S(1)} custom-call(f32[128,128]{1,0:T(8,128)S(1)} %convolution_subtract_fusion.8), custom_call_target="Cholesky" | custom-call | tf_op jit(solution)/shard_map/jit(cholesky)/cholesky | solution.py:31
  461.5 10.9 %while.1 = (s32[]{:T(128)}, f32[512,512]{1,0:T(8,128)S(1)}, s32[4,2]{0,1:T(2,128)S(1)}, f32[4,128,128]{2,1,0:T(8,128)}, s32[]{:T(128)}) while((s32[]{:T(128)}, f32[512,512]{1,0:T(8,128)S(1)}, s32[4,2]{0,1:T(2,128)S(1)}, f32[4,128,128]{2,1,0:T(8,128)}, s32[]{:T(128)}) %tuple.36), condition=%wide.while_cond, body=%wide.while_body.sunk | while | flops 2 | bytes 132705 | solution.py:33
  462.2 2.0 bitcast_dynamic-update-slice_fusion.2
  464.9 2.0 bitcast_dynamic-update-slice_fusion.2
  467.6 2.0 bitcast_dynamic-update-slice_fusion.2
  470.3 2.1 bitcast_dynamic-update-slice_fusion.2
  472.4 40.1 %custom-call.35 = f32[4,128,128]{1,2,0:T(8,128)S(1)} custom-call(f32[4,128,128]{2,1,0:T(8,128)} %get-tuple-element.10), custom_call_target="InvertDiagBlocksLowerTriangular" | custom-call | tf_op jit(solution)/shard_map/triangular_solve | solution.py:33
  512.5 1.2 fusion.33
  513.8 1.2 convolution_subtract_fusion.7
  515.2 1.2 convolution_subtract_fusion.4
  516.8 1.3 convolution_subtract_fusion.3
  520.7 0.9 fusion.2
  521.6 4.0 all-to-all-start
  525.7 1.0 convolution_divide_fusion
  526.6 5.8 %all-to-all-done = f32[4,128,256]{2,1,0:T(8,128)S(1)} async-done(((f32[4,128,256]{2,1,0:T(8,128)}), f32[4,128,256]{2,1,0:T(8,128)S(1)}, u32[]{:S(2)}, u32[]{:S(2)}) %all-to-all-start) | async-done | bytes 524320 | tf_op jit(solution)/shard_map/all_to_all | solution.py:44
  532.4 0.8 copy.11
  (58 shorter events, 12.0 us)
Async XLA Ops:
  7.2 16.4 %copy-start = (bf16[2048,256]{1,0:T(8,128)(2,1)S(1)}, bf16[2048,256]{1,0:T(8,128)(2,1)}, u32[]{:S(2)}) copy-start(bf16[2048,256]{1,0:T(8,128)(2,1)} %param.7) | copy-start | bytes 3145732
  7.2 367.0 %all-reduce.4.cloned.1.call-start = ((), (), s32[]{:S(2)}) async-start(), calls=%async_computation.1 | async-start | bytes 3145728 | tf_op jit(solution)/shard_map/psum | solution.py:30
  513.7 11.8 %copy-start.1 = (s32[8]{0:T(128)S(1)}, s32[8]{0:T(128)}, u32[]{:S(2)}) copy-start(s32[8]{0:T(128)} %param.9) | copy-start | bytes 100
  521.6 10.9 %all-to-all-start = ((f32[4,128,256]{2,1,0:T(8,128)}), f32[4,128,256]{2,1,0:T(8,128)S(1)}, u32[]{:S(2)}, u32[]{:S(2)}) async-start(f32[4,128,256]{2,1,0:T(8,128)} %bitcast.16), calls=%async_computation | async-start | bytes 1048576 | tf_op jit(solution)/shard_map/all_to_all | solution.py:44
Sparse Core Ops, SparseCore 0:
  25.2 348.9 all-reduce.3
where the time goes:
time: 543 us; the launch traced here: 540 us
  waiting for transfers between devices  355 us (65%)
  other arithmetic  127 us (23%)
  local copies, waits for them, and re-layouts  22.3 us (4%)
  between operations  16.9 us (3%)
  matrix products  14.7 us (3%)
    psum x1, waiting for transfers between devices, on_device(): gram, cross = lax.psum((gram_local, cross_local), 'samp')  349 us
    another operation x15, other arithmetic, on_device(): lower = jnp.linalg.cholesky(gram)  79.5 us
    another operation x3, other arithmetic, on_device(): lax.linalg.triangular_solve(lower, inner, left_side=True, lower=True, tra...  40.3 us
    another operation x12, local copies, waits for them, and re-layouts  10.9 us
  transfers between devices with their start and end apart: 2, of which 2 were waited for; matrix products, arithmetic and copies ran while one was open for 0% of the time, Pallas kernels for 0%

commit v1 on v0

v1 whole, which is shorter than its diff:
```python
import jax
import jax.numpy as jnp
from jax import lax
from jax.experimental import pallas as pl
from jax.experimental.pallas import tpu as pltpu
from jax.sharding import PartitionSpec as P

BLOCK = 64
GROUPS = 8
TERMS = 512
MESH = pl.DeviceIdType.MESH
F32 = jnp.float32
BF16 = jnp.bfloat16


def local_kernel(points_ref, yields_ref, term_ref, cross_ref, gram_ref, psi_ref):
    params, samples = points_ref.shape
    width = 3 * params
    lane = lax.broadcasted_iota(jnp.int32, (TERMS, 256), 1)

    def pick(column):
        degree = column & 3
        target = (degree - 1) * params + (column >> 2)
        hit = (lane == target) | (lane == target + width) | (lane == target + 2 * width)
        chosen = jnp.where(degree == 0, (lane == 3 * width).astype(F32), hit.astype(F32))
        return chosen.astype(BF16)

    pick_a = pick(term_ref[:, 0:1])
    pick_b = pick(term_ref[:, 1:2])
    step = 512
    for start in range(0, samples, step):
        xs = points_ref[:, start:start + step]
        first = 1.7320508075688772 * xs
        second = 2.23606797749979 * (1.5 * xs * xs - 0.5)
        third = 2.6457513110645907 * (2.5 * xs * xs * xs - 1.5 * xs)
        degrees = jnp.concatenate([first, second, third], axis=0)
        high = degrees.astype(BF16).astype(F32)
        rest = degrees - high
        middle = rest.astype(BF16).astype(F32)
        low = rest - middle
        table = jnp.concatenate(
            [high, middle, low, jnp.ones((8, step), F32), jnp.zeros((256 - 3 * width - 8, step), F32)], axis=0
        ).astype(BF16)
        left = jnp.dot(pick_a, table, preferred_element_type=F32)
        right = jnp.dot(pick_b, table, preferred_element_type=F32)
        psi_ref[:, start:start + step] = (left * right).astype(BF16)

    cross_ref[...] = jnp.dot(psi_ref[...], yields_ref[...], preferred_element_type=F32)

    cell = lax.axis_index("cell")
    low_half = cell < 2
    spots = (
        (0, 128, cell * 128, cell * 128),
        (128, 128, cell * 128, lax.rem(cell + 1, 4) * 128),
        (256, 64, jnp.where(low_half, cell * 128, cell * 128 - 192), jnp.where(low_half, cell * 128 + 256, cell * 128)),
    )
    for place, rows, a, b in spots:
        one = psi_ref[pl.ds(pl.multiple_of(a, 64), rows), :]
        two = psi_ref[pl.ds(pl.multiple_of(b, 128), 128), :]
        gram_ref[place:place + rows, :] = lax.dot_general(one, two, (((1,), (1,)), ((), ())), preferred_element_type=F32)


def local_products(points, yields, term_index):
    vmem = pl.BlockSpec(memory_space=pltpu.VMEM)
    return pl.pallas_call(
        local_kernel,
        out_shape=(jax.ShapeDtypeStruct((TERMS, yields.shape[1]), F32), jax.ShapeDtypeStruct((320, 128), F32)),
        in_specs=[vmem] * 3,
        out_specs=(vmem, vmem),
        scratch_shapes=[pltpu.VMEM((TERMS, points.shape[1]), BF16)],
        compiler_params=pltpu.CompilerParams(vmem_limit_bytes=48 << 20),
        name="local_products",
    )(points, yields, term_index)


def sum_kernel(cross_ref, gram_ref, cross_out, gram_out, r_core, s_core, r_y, s_y, r_zc, r_zg, a_z, send_sem, recv_sem):
    samp, cell = lax.axis_index("samp"), lax.axis_index("cell")
    core = lax.rem(samp, 2)
    y = lax.rem(samp // 2, 4)
    z = samp // 8

    def at(zz, yy, cc):
        return {"samp": (zz * 4 + yy) * 2 + cc, "cell": cell}

    def along_x(d):
        return {"samp": samp, "cell": lax.rem(cell + d, 4)}

    other = at(z, y, 1 - core)
    ys = [lax.rem(y + d, 4) for d in range(1, 4)]
    zs = [lax.rem(z + d, 16) for d in range(1, 16)]
    barrier = pltpu.get_barrier_semaphore()
    everyone = [other] + [at(z, v, core) for v in ys] + [at(v, y, core) for v in zs] + [along_x(d) for d in range(1, 4)]
    for device in everyone:
        pl.semaphore_signal(barrier, inc=1, device_id=device, device_id_type=MESH)
    pl.semaphore_wait(barrier, len(everyone))

    count = [0]
    started = []

    def send(src, dst, device):
        n = count[0]
        count[0] += 1
        copy = pltpu.make_async_remote_copy(
            src_ref=src, dst_ref=dst, send_sem=send_sem.at[n], recv_sem=recv_sem.at[n], device_id=device, device_id_type=MESH
        )
        return copy

    def go(src, dst, device):
        copy = send(src, dst, device)
        copy.start()
        started.append(copy)
        return copy

    far = pl.multiple_of((1 - core) * 128, 128)
    near = pl.multiple_of(core * 128, 128)
    first = []
    for q in range(4):
        first.append((
            go(cross_ref.at[q * 128:(q + 1) * 128, pl.ds(far, 128)], r_core.at[q, 0:128], other),
            go(gram_ref.at[pl.ds(pl.multiple_of((1 - core) * 160 + q * 40, 8), 40)], r_core.at[q, 128:168], other),
        ))
    for q in range(4):
        for copy in first[q]:
            copy.wait_recv()
        s_core[q, 0:128] = cross_ref[q * 128:(q + 1) * 128, pl.ds(near, 128)] + r_core[q, 0:128]
        s_core[q, 128:168] = gram_ref[pl.ds(pl.multiple_of(core * 160 + q * 40, 8), 40)] + r_core[q, 128:168]

    second = [go(s_core.at[v], r_y.at[d], at(z, v, core)) for d, v in enumerate(ys)]
    for copy in second:
        copy.wait_recv()
    s_y[...] = (s_core[y] + r_y[0]) + (r_y[1] + r_y[2])

    third = []
    extra = []
    for d, v in enumerate(zs):
        third.append(go(s_y.at[pl.ds(pl.multiple_of(v * 8, 8), 8)], r_zc.at[d], at(v, y, core)))
        copy = send(s_y.at[pl.ds(pl.multiple_of(128 + jnp.minimum(v, 4) * 8, 8), 8)], r_zg.at[d], at(v, y, core))
        extra.append(copy)
        pl.when(v < 5)(copy.start)
    for copy in third:
        copy.wait_recv()
    mine = pl.ds(pl.multiple_of(z * 8, 8), 8)
    total = s_y[mine]
    for d in range(15):
        total = total + r_zc[d]
    a_z[mine] = total
    fourth = [go(a_z.at[mine], a_z.at[mine], at(v, y, core)) for v in zs]
    mine_gram = pl.ds(pl.multiple_of(128 + jnp.minimum(z, 4) * 8, 8), 8)
    fourth_gram = [send(a_z.at[mine_gram], a_z.at[mine_gram], at(v, y, core)) for v in zs]

    @pl.when(z < 5)
    def _():
        for copy in extra:
            copy.wait_recv()
        total = s_y[mine_gram]
        for d in range(15):
            total = total + r_zg[d]
        a_z[mine_gram] = total
        for copy in fourth_gram:
            copy.start()

    for copy in fourth:
        copy.wait_recv()
    for d, copy in enumerate(fourth_gram):
        pl.when(lax.rem(z + 15 - d, 16) < 5)(copy.wait_recv)

    fifth = []
    cross_out[pl.ds(pl.multiple_of(y * 128, 128), 128), pl.ds(near, 128)] = a_z[0:128]
    gram_out[cell, pl.ds(pl.multiple_of(core * 160 + y * 40, 8), 40)] = a_z[128:168]
    for v in ys:
        fifth.append((
            go(a_z.at[128:168], gram_out.at[cell, pl.ds(pl.multiple_of(core * 160 + y * 40, 8), 40)], at(z, v, core)),
            go(a_z.at[0:128], cross_out.at[pl.ds(pl.multiple_of(y * 128, 128), 128), pl.ds(near, 128)], at(z, v, core)),
        ))
    for gram_copy, unused in fifth:
        gram_copy.wait_recv()
    half = pl.ds(pl.multiple_of(core * 160, 8), 160)
    sixth = [go(gram_out.at[cell, half], gram_out.at[cell, half], along_x(d)) for d in range(1, 4)]
    for unused, cross_copy in fifth:
        cross_copy.wait_recv()
    seventh = [go(cross_out.at[:, pl.ds(near, 128)], cross_out.at[:, pl.ds(near, 128)], other)]
    for copy in sixth:
        copy.wait_recv()
    seventh.append(go(gram_out.at[:, half], gram_out.at[:, half], other))
    for copy in seventh:
        copy.wait_recv()
    for copy in started:
        copy.wait_send()
    for d, v in enumerate(zs):
        pl.when(v < 5)(extra[d].wait_send)

    @pl.when(z < 5)
    def _():
        for copy in fourth_gram:
            copy.wait_send()


def sum_all(cross, gram):
    vmem = pl.BlockSpec(memory_space=pltpu.VMEM)
    copies = 8 + 3 + 30 + 30 + 6 + 3 + 2
    return pl.pallas_call(
        sum_kernel,
        out_shape=(jax.ShapeDtypeStruct(cross.shape, F32), jax.ShapeDtypeStruct((4, 320, 128), F32)),
        in_specs=[vmem] * 2,
        out_specs=(vmem, vmem),
        scratch_shapes=[
            pltpu.VMEM((4, 168, 128), F32),
            pltpu.VMEM((4, 168, 128), F32),
            pltpu.VMEM((3, 168, 128), F32),
            pltpu.VMEM((168, 128), F32),
            pltpu.VMEM((15, 8, 128), F32),
            pltpu.VMEM((15, 8, 128), F32),
            pltpu.VMEM((168, 128), F32),
            pltpu.SemaphoreType.DMA((copies,)),
            pltpu.SemaphoreType.DMA((copies,)),
        ],
        compiler_params=pltpu.CompilerParams(collective_id=0, has_side_effects=True, vmem_limit_bytes=32 << 20),
        name="sum_all",
    )(cross, gram)


def whole_gram(parts):
    diag = [parts[i, 0:128] for i in range(4)]
    next_one = [parts[i, 128:256] for i in range(4)]
    skip = [jnp.concatenate([parts[i, 256:320], parts[i + 2, 256:320]], axis=0) for i in range(2)]
    return jnp.block([
        [diag[0], next_one[0], skip[0], next_one[3].T],
        [next_one[0].T, diag[1], next_one[1], skip[1]],
        [skip[0].T, next_one[1].T, diag[2], next_one[2]],
        [next_one[3], skip[1].T, next_one[2].T, diag[3]],
    ])


def on_device(points, yields, term_index, block_group):
    cross_local, gram_local = local_products(points, yields, term_index)
    cross, gram_parts = sum_all(cross_local, gram_local)
    gram = whole_gram(gram_parts)
    lower = jnp.linalg.cholesky(gram)
    inner = lax.linalg.triangular_solve(lower, cross, left_side=True, lower=True)
    coef = lax.linalg.triangular_solve(lower, inner, left_side=True, lower=True, transpose_a=True)
    total_samples = points.shape[1] * lax.axis_size("samp")
    scaled = coef * jnp.sqrt(jnp.float32(total_samples))
    terms = coef.shape[0]
    keep = (jnp.arange(terms) >= 1).astype(jnp.float32)
    squares = coef * coef * keep[:, None]
    groups = jnp.repeat(block_group, BLOCK)
    member = (groups[None, :] == jnp.arange(GROUPS, dtype=jnp.int32)[:, None]).astype(jnp.float32)
    part = jnp.dot(member, squares, precision=lax.Precision.HIGHEST)
    total = jnp.sum(squares, axis=0)
    sobol = part / total[None, :]
    coefficients = lax.all_to_all(scaled, "cell", split_axis=0, concat_axis=1, tiled=True)
    return (coefficients, sobol)


def solution(mesh):
    placed = (P(None, "samp"), P("samp", "cell"), P(), P())
    return jax.shard_map(
        on_device,
        mesh=mesh,
        in_specs=placed,
        out_specs=(P("cell", None), P(None, "cell")),
        check_vma=False,
    )
```

time: 543 us -> 220 us (0.41)
  waiting for transfers between devices: 355 us -> 8.42 us
  Pallas kernels: 0 us -> 58.1 us
  between operations: 16.9 us -> 3.57 us
  matrix products: 14.7 us -> 7.25 us
  local copies, waits for them, and re-layouts: 22.3 us -> 15.6 us
    psum x1 -> x0, waiting for transfers between devices: 349 us -> none  [on_device(): gram, cross = lax.psum((gram_local, cross_local), 'samp')]
    pallas_call x0 -> x2, Pallas kernels: none -> 58.1 us  [the longest x1 55.3 us: sum_all(): pl.pallas_call(sum_kernel, out_shape=(jax.ShapeDtypeStruct(cross.shape, F...]
    gather x2 -> x0, local copies, waits for them, and re-layouts: 7.18 us -> none  [the longest x1 3.62 us: design(): left = jnp.take(table, term_index[:, 0], axis=0)]
    another operation x14 -> x12, local copies, waits for them, and re-layouts: 11.4 us -> 10.6 us
  transfers between devices with their start and end apart: 2 -> 1, of which waited for: 2 -> 1; matrix products, arithmetic and copies ran while one was open for 0% -> 1% of each run, Pallas kernels for 0% -> 0%
where the time goes in v1:
time: 220 us; the launch traced here: 219 us
  other arithmetic  123 us (56%)
  Pallas kernels  58.1 us (26%)
  local copies, waits for them, and re-layouts  15.6 us (7%)
  waiting for transfers between devices  8.42 us (4%)
  matrix products  7.25 us (3%)
  starting transfers between devices  3.6 us (2%)
  between operations  3.57 us (2%)
    another operation x15, other arithmetic, on_device(): lower = jnp.linalg.cholesky(gram)  79.5 us
    pallas_call x1, Pallas kernels, sum_all(): pl.pallas_call(sum_kernel, out_shape=(jax.ShapeDtypeStruct(cross.shape, F...  55.3 us
    another operation x3, other arithmetic, on_device(): lax.linalg.triangular_solve(lower, inner, left_side=True, lower=True, tra...  40.3 us
    another operation x12, local copies, waits for them, and re-layouts  10.6 us
    all_to_all x1, waiting for transfers between devices, on_device(): lax.all_to_all(scaled, 'cell', split_axis=0, concat_axis=1, tiled=True)  8.42 us
  transfers between devices with their start and end apart: 1, of which 1 were waited for; matrix products, arithmetic and copies ran while one was open for 1% of the time, Pallas kernels for 0%

profile of v1, /device:TPU:1, one launch (start us, length us, event | category | flops | bytes accessed | tf_op | source)
XLA Modules:
  0.0 219.4 jit_solution(1746081498711754046)
XLA Ops:
  0.6 0.9 copy.6.term_ref
  1.6 1.2 copy-done
  2.8 2.8 %local_products.1 = (f32[512,256]{1,0:T(8,128)S(1)}, f32[320,128]{1,0:T(8,128)S(1)}) custom-call(f32[24,2048]{1,0:T(8,128)S(1)} %copy-done.1, bf16[2048,256]{1,0:T(8,128)(2,1)S(1)} %copy-done, s32[512,2]{1,0:T(8,128)S(1)} %copy.6.term_ref), custom_call_target="tpu_custom_call" | custom-call | tf_op jit(solution)/shard_map/local_products/pallas_call | solution.py:65
  5.6 55.3 %sum_all.1 = (f32[512,256]{1,0:T(8,128)S(1)}, f32[4,320,128]{2,1,0:T(8,128)S(1)}) custom-call(f32[512,256]{1,0:T(8,128)S(1)} %get-tuple-element.6.cross_ref, f32[320,128]{1,0:T(8,128)S(1)} %get-tuple-element.7.gram_ref), custom_call_target="tpu_custom_call" | custom-call | tf_op jit(solution)/shard_map/sum_all/pallas_call | solution.py:201
  61.9 0.7 copy.14
  62.6 0.9 maximum_maximum_fusion
  63.9 1.1 fusion
  65.0 11.7 %cholesky.104 = f32[128,128]{1,0:T(8,128)S(1)} custom-call(f32[128,128]{1,0:T(8,128)S(1)} %cholesky.266), custom_call_target="Cholesky" | custom-call | tf_op jit(solution)/shard_map/jit(cholesky)/cholesky | solution.py:238
  76.9 9.8 %custom-call.32 = f32[1,128,128]{1,2,0:T(8,128)S(1)} custom-call(f32[1,128,128]{2,1,0:T(8,128)S(1)} %get-tuple-element.55), custom_call_target="InvertDiagBlocksLowerTriangular" | custom-call | tf_op jit(solution)/shard_map/jit(cholesky)/cholesky | solution.py:238
  87.4 11.8 %cholesky.217 = f32[128,128]{1,0:T(8,128)S(1)} custom-call(f32[128,128]{1,0:T(8,128)S(1)} %cholesky.270), custom_call_target="Cholesky" | custom-call | tf_op jit(solution)/shard_map/jit(cholesky)/cholesky | solution.py:238
  99.3 0.6 compare_reduce_fusion.2
  99.9 0.7 compare_reduce_fusion.3
  100.6 9.8 %custom-call.33 = f32[1,128,128]{1,2,0:T(8,128)S(1)} custom-call(f32[1,128,128]{2,1,0:T(8,128)S(1)} %get-tuple-element.52), custom_call_target="InvertDiagBlocksLowerTriangular" | custom-call | tf_op jit(solution)/shard_map/jit(cholesky)/cholesky | solution.py:238
  111.1 11.7 %cholesky.238 = f32[128,128]{1,0:T(8,128)S(1)} custom-call(f32[128,128]{1,0:T(8,128)S(1)} %cholesky.275), custom_call_target="Cholesky" | custom-call | tf_op jit(solution)/shard_map/jit(cholesky)/cholesky | solution.py:238
  122.8 0.7 compare_reduce_fusion.1
  123.5 9.8 %custom-call.34 = f32[1,128,128]{1,2,0:T(8,128)S(1)} custom-call(f32[1,128,128]{2,1,0:T(8,128)S(1)} %get-tuple-element.49), custom_call_target="InvertDiagBlocksLowerTriangular" | custom-call | tf_op jit(solution)/shard_map/jit(cholesky)/cholesky | solution.py:238
  133.9 12.0 %cholesky.255 = f32[128,128]{1,0:T(8,128)S(1)} custom-call(f32[128,128]{1,0:T(8,128)S(1)} %convolution_subtract_fusion.8), custom_call_target="Cholesky" | custom-call | tf_op jit(solution)/shard_map/jit(cholesky)/cholesky | solution.py:238
  145.9 0.7 compare_reduce_fusion
  149.3 10.6 %while.1 = (s32[]{:T(128)}, f32[512,512]{1,0:T(8,128)S(1)}, s32[4,2]{0,1:T(2,128)S(1)}, f32[4,128,128]{2,1,0:T(8,128)}, s32[]{:T(128)}) while((s32[]{:T(128)}, f32[512,512]{1,0:T(8,128)S(1)}, s32[4,2]{0,1:T(2,128)S(1)}, f32[4,128,128]{2,1,0:T(8,128)}, s32[]{:T(128)}) %tuple.44), condition=%wide.while_cond, body=%wide.while_body.sunk | while | flops 2 | bytes 132705 | solution.py:240
  149.4 0.6 fusion.64
  150.0 2.0 bitcast_dynamic-update-slice_fusion.2
  152.0 0.6 fusion.64
  152.6 2.0 bitcast_dynamic-update-slice_fusion.2
  154.7 0.6 fusion.64
  155.3 2.0 bitcast_dynamic-update-slice_fusion.2
  157.9 2.0 bitcast_dynamic-update-slice_fusion.2
  159.9 40.1 %custom-call.35 = f32[4,128,128]{1,2,0:T(8,128)S(1)} custom-call(f32[4,128,128]{2,1,0:T(8,128)} %get-tuple-element.17), custom_call_target="InvertDiagBlocksLowerTriangular" | custom-call | tf_op jit(solution)/shard_map/triangular_solve | solution.py:240
  204.5 0.9 fusion.1
  205.4 3.6 %all-to-all-start = ((f32[4,128,256]{2,1,0:T(8,128)}), f32[4,128,256]{2,1,0:T(8,128)S(1)}, u32[]{:S(2)}, u32[]{:S(2)}) async-start(f32[4,128,256]{2,1,0:T(8,128)} %bitcast.29), calls=%async_computation | async-start | bytes 1048576 | tf_op jit(solution)/shard_map/all_to_all | solution.py:251
  209.2 1.0 convolution_divide_fusion
  210.2 8.4 %all-to-all-done = f32[4,128,256]{2,1,0:T(8,128)S(1)} async-done(((f32[4,128,256]{2,1,0:T(8,128)}), f32[4,128,256]{2,1,0:T(8,128)S(1)}, u32[]{:S(2)}, u32[]{:S(2)}) %all-to-all-start) | async-done | bytes 524320 | tf_op jit(solution)/shard_map/all_to_all | solution.py:251
  218.6 0.9 copy.19
  (61 shorter events, 9.0 us)
Async XLA Ops:
  0.6 0.9 copy-start.1
  1.6 1.2 copy-start
  61.3 1.3 copy-start.2
  61.3 1.3 copy-start.3
  205.4 3.6 %copy-start.4 = (s32[8]{0:T(128)S(1)}, s32[8]{0:T(128)}, u32[]{:S(2)}) copy-start(s32[8]{0:T(128)} %param.7) | copy-start | bytes 100
  205.4 13.2 %all-to-all-start = ((f32[4,128,256]{2,1,0:T(8,128)}), f32[4,128,256]{2,1,0:T(8,128)S(1)}, u32[]{:S(2)}, u32[]{:S(2)}) async-start(f32[4,128,256]{2,1,0:T(8,128)} %bitcast.29), calls=%async_computation | async-start | bytes 1048576 | tf_op jit(solution)/shard_map/all_to_all | solution.py:251

commit v2 on v1

--- a/solution.py
+++ b/solution.py
@@ -1,3 +1,5 @@
+import functools
+
 import jax
 import jax.numpy as jnp
 from jax import lax
@@ -5,9 +7,9 @@
 from jax.experimental.pallas import tpu as pltpu
 from jax.sharding import PartitionSpec as P
 
-BLOCK = 64
 GROUPS = 8
 TERMS = 512
+HI = lax.Precision.HIGHEST
 MESH = pl.DeviceIdType.MESH
 F32 = jnp.float32
 BF16 = jnp.bfloat16
@@ -51,7 +53,7 @@
     low_half = cell < 2
     spots = (
         (0, 128, cell * 128, cell * 128),
-        (128, 128, cell * 128, lax.rem(cell + 1, 4) * 128),
+        (128, 128, jnp.where(cell == 3, 0, cell * 128), jnp.minimum(cell + 1, 3) * 128),
         (256, 64, jnp.where(low_half, cell * 128, cell * 128 - 192), jnp.where(low_half, cell * 128 + 256, cell * 128)),
     )
     for place, rows, a, b in spots:
@@ -219,37 +221,185 @@
     )(cross, gram)
 
 
-def whole_gram(parts):
-    diag = [parts[i, 0:128] for i in range(4)]
-    next_one = [parts[i, 128:256] for i in range(4)]
-    skip = [jnp.concatenate([parts[i, 256:320], parts[i + 2, 256:320]], axis=0) for i in range(2)]
-    return jnp.block([
-        [diag[0], next_one[0], skip[0], next_one[3].T],
-        [next_one[0].T, diag[1], next_one[1], skip[1]],
-        [skip[0].T, next_one[1].T, diag[2], next_one[2]],
-        [next_one[3], skip[1].T, next_one[2].T, diag[3]],
-    ])
+def full(row):
+    return jnp.broadcast_to(row, (8, 128))
+
+
+def sweep_rows(rows, p, lane, sub):
+    pivot = rows[p]
+    at = 8 * p
+    inside = (lane >= at) & (lane < at + 8)
+    spread = [full(pivot[:, at + j:at + j + 1]) for j in range(8)]
+    m = [[None] * 8 for _ in range(8)]
+    for j in range(8):
+        for i in range(j + 1):
+            m[i][j] = full(spread[j][i:i + 1, :])
+    for k in range(8):
+        r = 1.0 / m[k][k]
+        t = [None if j == k else m[min(j, k)][max(j, k)] * r for j in range(8)]
+        old = [m[min(j, k)][max(j, k)] for j in range(8)]
+        for j in range(8):
+            for i in range(j + 1):
+                if i != k and j != k:
+                    m[i][j] = m[i][j] - old[i] * t[j]
+        for j in range(8):
+            if j != k:
+                m[min(j, k)][max(j, k)] = t[j]
+        m[k][k] = -r
+    target = jnp.where(inside, jnp.where(lane - at == sub, 1.0, 0.0), -pivot)
+    source = [full(target[i:i + 1, :]) for i in range(8)]
+    wide = []
+    for j in range(8):
+        terms = [m[min(i, j)][max(i, j)] * source[i] for i in range(8)]
+        wide.append(((terms[0] + terms[1]) + (terms[2] + terms[3])) + ((terms[4] + terms[5]) + (terms[6] + terms[7])))
+    out = [None] * 16
+    order = [(p + 1 + q) % 16 for q in range(15)]
+    for q in order:
+        terms = [full(rows[q][:, at + j:at + j + 1]) * wide[j] for j in range(8)]
+        total = ((terms[0] + terms[1]) + (terms[2] + terms[3])) + ((terms[4] + terms[5]) + (terms[6] + terms[7]))
+        out[q] = jnp.where(inside, 0.0, rows[q]) - total
+    packed = wide[7]
+    for j in range(7):
+        packed = jnp.where(sub == j, wide[j], packed)
+    out[p] = packed
+    return out
+
+
+def solve_kernel(scale, cross_ref, gram_ref, group_ref, coef_ref, sobol_ref, a_ref, d_ref):
+    cells = cross_ref.shape[1]
+    lane = lax.broadcasted_iota(jnp.int32, (8, 128), 1)
+    sub = lax.broadcasted_iota(jnp.int32, (8, 128), 0)
+    for b in range(4):
+        a_ref[b, :, 128 * b:128 * b + 128] = gram_ref[b, 0:128]
+        a_ref[b, :, 512:512 + cells] = cross_ref[128 * b:128 * b + 128]
+    for b in range(3):
+        a_ref[b, :, 128 * b + 128:128 * b + 256] = gram_ref[b, 128:256]
+    a_ref[0, :, 384:512] = gram_ref[3, 128:256]
+    for b in range(2):
+        a_ref[b, 0:64, 128 * b + 256:128 * b + 384] = gram_ref[b, 256:320]
+        a_ref[b, 64:128, 128 * b + 256:128 * b + 384] = gram_ref[b + 2, 256:320]
+    end = 512 + cells
+    d_ref[...] = a_ref[0, :, 0:128]
+
+    def block(b, unused):
+        rows = [d_ref[8 * i:8 * i + 8, :] for i in range(16)]
+        for p in range(16):
+            rows = sweep_rows(rows, p, lane, sub)
+        for i in range(16):
+            d_ref[8 * i:8 * i + 8, :] = -rows[i]
+        for s in range(4):
+            @pl.when(b == s)
+            def _():
+                begin = 128 * s + 128
+                w = jnp.dot(d_ref[...], a_ref[s, :, begin:end], precision=HI, preferred_element_type=F32)
+                for i in range(s + 1, 4):
+                    here = slice(128 * i, end)
+                    a_ref[i, :, here] -= lax.dot_general(
+                        a_ref[s, :, 128 * i:128 * i + 128], w[:, 128 * i - begin:], (((0,), (0,)), ((), ())), precision=HI, preferred_element_type=F32)
+                a_ref[s, :, begin:end] = w
+                if s < 3:
+                    d_ref[...] = a_ref[s + 1, :, begin:begin + 128]
+        return unused
+
+    lax.fori_loop(0, 4, block, 0)
+    found = [None] * 4
+    for b in (3, 2, 1, 0):
+        x = a_ref[b, :, 512:end]
+        if b < 3:
+            below = jnp.concatenate(found[b + 1:], axis=0)
+            x = x - jnp.dot(a_ref[b, :, 128 * b + 128:512], below, precision=HI, preferred_element_type=F32)
+        found[b] = x
+    sums = []
+    for b in range(4):
+        x = found[b]
+        coef_ref[128 * b:128 * b + 128] = x * scale
+        sq = x * x
+        if b == 0:
+            sq = jnp.where(lax.broadcasted_iota(jnp.int32, sq.shape, 0) == 0, 0.0, sq)
+        sums.append(jnp.sum(sq[0:64], axis=0, keepdims=True))
+        sums.append(jnp.sum(sq[64:128], axis=0, keepdims=True))
+    total = sums[0]
+    for s in sums[1:]:
+        total = total + s
+    for g in range(GROUPS):
+        part = jnp.zeros_like(total)
+        for b in range(8):
+            part = part + jnp.where(group_ref[b] == g, sums[b], 0.0)
+        sobol_ref[g:g + 1] = part / total
+
+
+def solve(cross, gram, block_group, scale):
+    vmem = pl.BlockSpec(memory_space=pltpu.VMEM)
+    cells = cross.shape[1]
+    return pl.pallas_call(
+        functools.partial(solve_kernel, scale),
+        out_shape=(jax.ShapeDtypeStruct(cross.shape, F32), jax.ShapeDtypeStruct((GROUPS, cells), F32)),
+        in_specs=[vmem, vmem, pl.BlockSpec(memory_space=pltpu.SMEM)],
+        out_specs=(vmem, vmem),
+        scratch_shapes=[pltpu.VMEM((4, 128, 512 + cells), F32), pltpu.VMEM((128, 128), F32)],
+        compiler_params=pltpu.CompilerParams(vmem_limit_bytes=32 << 20),
+        name="solve",
+    )(cross, gram, block_group)
+
+
+def exchange_kernel(coef_ref, out_ref, send_sem, recv_sem):
+    samp, cell = lax.axis_index("samp"), lax.axis_index("cell")
+    core = lax.rem(samp, 2)
+    width = coef_ref.shape[1]
+    rows = out_ref.shape[0]
+    half = width // 2
+    other = {"samp": samp + 1 - 2 * core, "cell": cell}
+    distances = (2, 1, 3)
+    peers = [lax.rem(cell + d, 4) for d in distances]
+    barrier = pltpu.get_barrier_semaphore()
+    for device in [other] + [{"samp": samp, "cell": v} for v in peers]:
+        pl.semaphore_signal(barrier, inc=1, device_id=device, device_id_type=MESH)
+    pl.semaphore_wait(barrier, 4)
+    side = pl.ds(pl.multiple_of(core * half, 128), half)
+    copies = []
+    for n, v in enumerate(peers):
+        copies.append(pltpu.make_async_remote_copy(
+            src_ref=coef_ref.at[pl.ds(pl.multiple_of(v * rows, 8), rows), side],
+            dst_ref=out_ref.at[:, pl.ds(pl.multiple_of(cell * width + core * half, 128), half)],
+            send_sem=send_sem.at[n], recv_sem=recv_sem.at[n],
+            device_id={"samp": samp, "cell": v}, device_id_type=MESH))
+        copies[-1].start()
+    out_ref[:, pl.ds(pl.multiple_of(cell * width, 128), width)] = coef_ref[pl.ds(pl.multiple_of(cell * rows, 8), rows), :]
+    passed = []
+    for n, d in ((1, 1), (2, 3), (0, 2)):
+        source = lax.rem(cell + 4 - d, 4)
+        copies[n].wait_recv()
+        piece = out_ref.at[:, pl.ds(pl.multiple_of(source * width + core * half, 128), half)]
+        passed.append(pltpu.make_async_remote_copy(
+            src_ref=piece, dst_ref=piece, send_sem=send_sem.at[3 + n], recv_sem=recv_sem.at[3 + n],
+            device_id=other, device_id_type=MESH))
+        passed[-1].start()
+    for copy in passed:
+        copy.wait_recv()
+    for copy in copies + passed:
+        copy.wait_send()
+
+
+def exchange(coef):
+    vmem = pl.BlockSpec(memory_space=pltpu.VMEM)
+    terms, cells = coef.shape
+    return pl.pallas_call(
+        exchange_kernel,
+        out_shape=jax.ShapeDtypeStruct((terms // 4, cells * 4), F32),
+        in_specs=[vmem],
+        out_specs=vmem,
+        scratch_shapes=[pltpu.SemaphoreType.DMA((6,)), pltpu.SemaphoreType.DMA((6,))],
+        compiler_params=pltpu.CompilerParams(collective_id=1, has_side_effects=True),
+        name="exchange",
+    )(coef)
 
 
 def on_device(points, yields, term_index, block_group):
     cross_local, gram_local = local_products(points, yields, term_index)
-    cross, gram_parts = sum_all(cross_local, gram_local)
-    gram = whole_gram(gram_parts)
-    lower = jnp.linalg.cholesky(gram)
-    inner = lax.linalg.triangular_solve(lower, cross, left_side=True, lower=True)
-    coef = lax.linalg.triangular_solve(lower, inner, left_side=True, lower=True, transpose_a=True)
+    cross, gram = sum_all(cross_local, gram_local)
     total_samples = points.shape[1] * lax.axis_size("samp")
-    scaled = coef * jnp.sqrt(jnp.float32(total_samples))
-    terms = coef.shape[0]
-    keep = (jnp.arange(terms) >= 1).astype(jnp.float32)
-    squares = coef * coef * keep[:, None]
-    groups = jnp.repeat(block_group, BLOCK)
-    member = (groups[None, :] == jnp.arange(GROUPS, dtype=jnp.int32)[:, None]).astype(jnp.float32)
-    part = jnp.dot(member, squares, precision=lax.Precision.HIGHEST)
-    total = jnp.sum(squares, axis=0)
-    sobol = part / total[None, :]
-    coefficients = lax.all_to_all(scaled, "cell", split_axis=0, concat_axis=1, tiled=True)
-    return (coefficients, sobol)
+    scaled, sobol = solve(cross, gram, block_group, float(total_samples) ** 0.5)
+    return (exchange(scaled), sobol)
 
 
 def solution(mesh):

time: 220 us -> 98.2 us (0.45)
  other arithmetic: 123 us -> 0 us
  Pallas kernels: 58.1 us -> 91.7 us
  local copies, waits for them, and re-layouts: 15.6 us -> 5.48 us
  waiting for transfers between devices: 8.42 us -> 0 us
  matrix products: 7.25 us -> 0 us
  starting transfers between devices: 3.6 us -> 0 us
  between operations: 3.57 us -> 0.67 us
    another operation x18 -> x0, other arithmetic: 120 us -> none  [the longest x15 79.5 us: on_device(): lower = jnp.linalg.cholesky(gram)]
    pallas_call x0 -> x2, Pallas kernels: none -> 33.6 us  [the longest x1 22.9 us: solve(): pl.pallas_call(functools.partial(solve_kernel, scale), out_shape=(jax.Sha...]
    another operation x17 -> x0, local copies, waits for them, and re-layouts: 10.7 us -> none
    all_to_all x1 -> x0, waiting for transfers between devices: 8.42 us -> none  [on_device(): lax.all_to_all(scaled, 'cell', split_axis=0, concat_axis=1, tiled=True)]
    another operation x20 -> x0, matrix products: 6.27 us -> none  [the longest x7 2.24 us: on_device(): lax.linalg.triangular_solve(lower, inner, left_side=True, lower=True, tra...]
    all_to_all x1 -> x0, starting transfers between devices: 3.6 us -> none  [on_device(): lax.all_to_all(scaled, 'cell', split_axis=0, concat_axis=1, tiled=True)]
    unnamed x11 -> x10, local copies, waits for them, and re-layouts: 2.16 us -> 5.48 us
  transfers between devices with their start and end apart: 1 -> 0, of which waited for: 1 -> 0; matrix products, arithmetic and copies ran while one was open for 1% -> 0% of each run, Pallas kernels for 0% -> 0%
where the time goes in v2:
time: 98.2 us; the launch traced here: 97.9 us
  Pallas kernels  91.7 us (93%)
  local copies, waits for them, and re-layouts  5.48 us (6%)
    pallas_call x1, Pallas kernels, sum_all(): pl.pallas_call(sum_kernel, out_shape=(jax.ShapeDtypeStruct(cross.shape, F...  55.3 us
    pallas_call x1, Pallas kernels, solve(): pl.pallas_call(functools.partial(solve_kernel, scale), out_shape=(jax.Sha...  22.9 us
    pallas_call x1, Pallas kernels, exchange(): pl.pallas_call(exchange_kernel, out_shape=jax.ShapeDtypeStruct((terms //...  10.7 us
    unnamed x10, local copies, waits for them, and re-layouts  5.48 us
    pallas_call x1, Pallas kernels, local_products(): pl.pallas_call(local_kernel, out_shape=(jax.ShapeDtypeStruct((TERMS, yiel...  2.81 us

profile of v2, /device:TPU:1, one launch (start us, length us, event | category | flops | bytes accessed | tf_op | source)
XLA Modules:
  0.0 97.9 jit_solution(10750420087639084931)
XLA Ops:
  0.6 0.0 copy-start.2
  0.6 0.9 copy.6.term_ref
  1.5 0.1 copy-done.2
  1.6 0.0 copy-start
  1.6 1.2 %copy-done = bf16[2048,256]{1,0:T(8,128)(2,1)S(1)} copy-done((bf16[2048,256]{1,0:T(8,128)(2,1)S(1)}, bf16[2048,256]{1,0:T(8,128)(2,1)}, u32[]{:S(2)}) %copy-start) | copy-done | bytes 1048600
  2.8 2.8 %local_products.1 = (f32[512,256]{1,0:T(8,128)S(1)}, f32[320,128]{1,0:T(8,128)S(1)}) custom-call(f32[24,2048]{1,0:T(8,128)S(1)} %copy-done.2, bf16[2048,256]{1,0:T(8,128)(2,1)S(1)} %copy-done, s32[512,2]{1,0:T(8,128)S(1)} %copy.6.term_ref), custom_call_target="tpu_custom_call" | custom-call | tf_op jit(solution)/shard_map/local_products/pallas_call | solution.py:67
  5.6 55.3 %sum_all.1 = (f32[512,256]{1,0:T(8,128)S(1)}, f32[4,320,128]{2,1,0:T(8,128)S(1)}) custom-call(f32[512,256]{1,0:T(8,128)S(1)} %get-tuple-element.8.cross_ref, f32[320,128]{1,0:T(8,128)S(1)} %get-tuple-element.9.gram_ref), custom_call_target="tpu_custom_call" | custom-call | tf_op jit(solution)/shard_map/sum_all/pallas_call | solution.py:203
  61.0 0.0 copy-start.3
  61.0 0.6 copy-done.3
  61.6 22.9 %solve.1 = (f32[512,256]{1,0:T(8,128)S(1)}, f32[8,256]{1,0:T(8,128)}) custom-call(f32[512,256]{1,0:T(8,128)S(1)} %get-tuple-element.10.cross_ref, f32[4,320,128]{2,1,0:T(8,128)S(1)} %get-tuple-element.11.gram_ref, s32[8]{0:T(128)S(1)} %copy-done.3), custom_call_target="tpu_custom_call" | custom-call | tf_op jit(solution)/shard_map/solve/pallas_call | solution.py:334
  84.5 0.0 copy-start.1
  84.5 0.8 copy-done.1
  85.3 10.7 %exchange.1 = f32[128,1024]{1,0:T(8,128)} custom-call(f32[512,256]{1,0:T(8,128)} %copy-done.1), custom_call_target="tpu_custom_call" | custom-call | tf_op jit(solution)/shard_map/exchange/pallas_call | solution.py:386
  96.0 1.9 %copy.8 = f32[128,1024]{1,0:T(8,128)} copy(f32[128,1024]{1,0:T(8,128)} %exchange.1) | data formatting | bytes 1048576
Async XLA Ops:
  0.6 0.9 copy-start.2
  1.6 1.2 %copy-start = (bf16[2048,256]{1,0:T(8,128)(2,1)S(1)}, bf16[2048,256]{1,0:T(8,128)(2,1)}, u32[]{:S(2)}) copy-start(bf16[2048,256]{1,0:T(8,128)(2,1)} %yields_ref.1) | copy-start | bytes 3145732
  61.0 0.7 copy-start.3
  84.5 0.8 copy-start.1

commit v3 on v0

v3 whole, which is shorter than its diff:
```python
import jax
import jax.numpy as jnp
from jax import lax
from jax.experimental import pallas as pl
from jax.experimental.pallas import tpu as pltpu
from jax.sharding import PartitionSpec as P

GROUPS = 8
TERMS = 512
HI = lax.Precision.HIGHEST
MESH = pl.DeviceIdType.MESH
F32 = jnp.float32
BF16 = jnp.bfloat16


def tile(start, size):
    return pl.ds(pl.multiple_of(start, 8), size)


def lanes(start, size):
    return pl.ds(pl.multiple_of(start, 128), size)


def basis(terms_ref, points_ref, psi_ref):
    params, samples = points_ref.shape
    width = 3 * params
    place = lax.broadcasted_iota(jnp.int32, (256, TERMS), 0)

    def pick(column):
        degree = column & 3
        target = (degree - 1) * params + (column >> 2)
        hit = (place == target) | (place == target + width) | (place == target + 2 * width)
        chosen = jnp.where(degree == 0, (place == 3 * width).astype(F32), hit.astype(F32))
        return chosen.T.astype(BF16)

    pick_a = pick(terms_ref[0:1, :])
    pick_b = pick(terms_ref[1:2, :])
    step = 512
    for start in range(0, samples, step):
        xs = points_ref[:, start:start + step]
        first = 1.7320508075688772 * xs
        second = 2.23606797749979 * (1.5 * xs * xs - 0.5)
        third = 2.6457513110645907 * (2.5 * xs * xs * xs - 1.5 * xs)
        degrees = jnp.concatenate([first, second, third], axis=0)
        high = degrees.astype(BF16).astype(F32)
        rest = degrees - high
        middle = rest.astype(BF16).astype(F32)
        low = rest - middle
        table = jnp.concatenate(
            [high, middle, low, jnp.ones((8, step), F32), jnp.zeros((256 - 3 * width - 8, step), F32)], axis=0
        ).astype(BF16)
        left = jnp.dot(pick_a, table, preferred_element_type=F32)
        right = jnp.dot(pick_b, table, preferred_element_type=F32)
        psi_ref[:, start:start + step] = (left * right).astype(BF16)


def gram_quarter(cell, psi_ref, gram_ref):
    low_half = cell < 2
    spots = (
        (0, 128, cell * 128, cell * 128),
        (128, 128, jnp.where(cell == 3, 0, cell * 128), jnp.minimum(cell + 1, 3) * 128),
        (256, 64, jnp.where(low_half, cell * 128, cell * 128 - 192), jnp.where(low_half, cell * 128 + 256, cell * 128)),
    )
    for place, rows, a, b in spots:
        one = psi_ref[pl.ds(pl.multiple_of(a, 64), rows), :]
        two = psi_ref[pl.ds(pl.multiple_of(b, 128), 128), :]
        gram_ref[place:place + rows, :] = lax.dot_general(one, two, (((1,), (1,)), ((), ())), preferred_element_type=F32)


def full(row):
    return jnp.broadcast_to(row, (8, 128))


def sweep_rows(rows, p, lane, sub):
    pivot = rows[p]
    at = 8 * p
    inside = (lane >= at) & (lane < at + 8)
    spread = [full(pivot[:, at + j:at + j + 1]) for j in range(8)]
    m = [[None] * 8 for _ in range(8)]
    for j in range(8):
        for i in range(j + 1):
            m[i][j] = full(spread[j][i:i + 1, :])
    for k in range(8):
        r = 1.0 / m[k][k]
        t = [None if j == k else m[min(j, k)][max(j, k)] * r for j in range(8)]
        old = [m[min(j, k)][max(j, k)] for j in range(8)]
        for j in range(8):
            for i in range(j + 1):
                if i != k and j != k:
                    m[i][j] = m[i][j] - old[i] * t[j]
        for j in range(8):
            if j != k:
                m[min(j, k)][max(j, k)] = t[j]
        m[k][k] = -r
    target = jnp.where(inside, jnp.where(lane - at == sub, 1.0, 0.0), -pivot)
    source = [full(target[i:i + 1, :]) for i in range(8)]
    wide = []
    for j in range(8):
        terms = [m[min(i, j)][max(i, j)] * source[i] for i in range(8)]
        wide.append(((terms[0] + terms[1]) + (terms[2] + terms[3])) + ((terms[4] + terms[5]) + (terms[6] + terms[7])))
    out = [None] * 16
    order = [(p + 1 + q) % 16 for q in range(15)]
    for q in order:
        terms = [full(rows[q][:, at + j:at + j + 1]) * wide[j] for j in range(8)]
        total = ((terms[0] + terms[1]) + (terms[2] + terms[3])) + ((terms[4] + terms[5]) + (terms[6] + terms[7]))
        out[q] = jnp.where(inside, 0.0, rows[q]) - total
    packed = wide[7]
    for j in range(7):
        packed = jnp.where(sub == j, wide[j], packed)
    out[p] = packed
    return out


def place_gram(gram_ref, a_ref):
    for b in range(4):
        a_ref[b, :, 128 * b:128 * b + 128] = gram_ref[b, 0:128]
    for b in range(3):
        a_ref[b, :, 128 * b + 128:128 * b + 256] = gram_ref[b, 128:256]
    a_ref[0, :, 384:512] = gram_ref[3, 128:256]
    for b in range(2):
        a_ref[b, 0:64, 128 * b + 256:128 * b + 384] = gram_ref[b, 256:320]
        a_ref[b, 64:128, 128 * b + 256:128 * b + 384] = gram_ref[b + 2, 256:320]


def fit_kernel(
    points_hbm, yields_hbm, terms_hbm, group_hbm, coef_out, share_out,
    points_ref, yields_ref, terms_ref, group_ref, psi_ref, cross_ref, gram_ref,
    got_gram, got_cross, half_gram, half_cross, y_gram, y_cross, part_gram, part_cross, z_gram, z_cross,
    all_gram, all_cross, whole_gram, whole_cross, a_ref, d_ref, x_ref,
    load_sem, core_s, core_r, y_s, y_r, zg_s, zg_r, zc_s, zc_r, bg_s, bg_r, bc_s, bc_r, yx_s, yx_r, yc_s, yc_r, x_s, x_r, f_s, f_r,
):
    samp, cell = lax.axis_index("samp"), lax.axis_index("cell")
    core = lax.rem(samp, 2)
    y = lax.rem(samp // 2, 4)
    z = samp // 8

    def at(zz, yy, cc, xx):
        return {"samp": (zz * 4 + yy) * 2 + cc, "cell": xx}

    def turn(v, d, n):
        return lax.rem(v + d, n)

    other = at(z, y, 1 - core, cell)
    far = (8, 7, 9, 6, 10, 5, 11, 4, 12, 3, 13, 2, 14, 1, 15)
    plane = [(dy, dx) for dy in (2, 1, 3, 0) for dx in (2, 1, 3, 0) if (dy, dx) != (0, 0)]
    barrier = pltpu.get_barrier_semaphore()
    greet = [at(turn(z, d, 16), y, core, cell) for d in far]
    greet += [at(z, turn(y, dy, 4), core, turn(cell, dx, 4)) for dy, dx in plane]
    greet += [other]
    for device in greet:
        pl.semaphore_signal(barrier, inc=1, device_id=device, device_id_type=MESH)

    loads = [
        pltpu.make_async_copy(terms_hbm, terms_ref, load_sem.at[0]),
        pltpu.make_async_copy(points_hbm, points_ref, load_sem.at[1]),
        pltpu.make_async_copy(yields_hbm, yields_ref, load_sem.at[2]),
        pltpu.make_async_copy(group_hbm, group_ref, load_sem.at[3]),
    ]
    for copy in loads:
        copy.start()
    loads[0].wait()
    loads[1].wait()
    basis(terms_ref, points_ref, psi_ref)
    gram_quarter(cell, psi_ref, gram_ref)
    loads[2].wait()
    cross_ref[...] = jnp.dot(psi_ref[...], yields_ref[...], preferred_element_type=F32)
    loads[3].wait()
    pl.semaphore_wait(barrier, len(greet))

    sent = []

    def remote(src, dst, s, r, device):
        return pltpu.make_async_remote_copy(
            src_ref=src, dst_ref=dst, send_sem=s, recv_sem=r, device_id=device, device_id_type=MESH)

    def go(*args):
        copy = remote(*args)
        copy.start()
        sent.append(copy)
        return copy

    def arrive(copies):
        for copy in copies:
            copy.wait_recv()

    core_g = go(gram_ref.at[tile((1 - core) * 160, 160)], got_gram, core_s.at[0], core_r.at[0], other)
    core_c = go(cross_ref.at[:, lanes((1 - core) * 128, 128)], got_cross, core_s.at[1], core_r.at[1], other)
    core_g.wait_recv()
    half_gram[...] = gram_ref[tile(core * 160, 160)] + got_gram[...]
    steps = (2, 1, 3)
    along_g = [
        go(half_gram.at[tile(turn(y, d, 4) * 40, 40)], y_gram.at[d - 1], y_s.at[d - 1], y_r.at[d - 1], at(z, turn(y, d, 4), core, cell))
        for d in steps]
    core_c.wait_recv()
    half_cross[...] = cross_ref[:, lanes(core * 128, 128)] + got_cross[...]
    along_c = [
        go(half_cross.at[tile(turn(y, d, 4) * 128, 128)], y_cross.at[d - 1], y_s.at[d + 2], y_r.at[d + 2], at(z, turn(y, d, 4), core, cell))
        for d in steps]

    arrive(along_g)
    part_gram[...] = (half_gram[tile(y * 40, 40)] + y_gram[0]) + (y_gram[1] + y_gram[2])
    to_owner = []
    for v in range(5):
        slot = lax.rem(z + 31 - v, 16)
        copy = remote(part_gram.at[8 * v:8 * v + 8], z_gram.at[jnp.minimum(slot, 14)], zg_s.at[v], zg_r.at[jnp.minimum(slot, 14)], at(v, y, core, cell))
        to_owner.append(copy)
        pl.when(z != v)(copy.start)
    arrive(along_c)
    part_cross[...] = (half_cross[tile(y * 128, 128)] + y_cross[0]) + (y_cross[1] + y_cross[2])
    z_c = [
        go(part_cross.at[tile(turn(z, d, 16) * 8, 8)], z_cross.at[d - 1], zc_s.at[d - 1], zc_r.at[d - 1], at(turn(z, d, 16), y, core, cell))
        for d in far]
    mine = tile(z * 8, 8)
    owned = tile(jnp.minimum(z, 4) * 8, 8)
    back_g = [
        remote(all_gram.at[owned], all_gram.at[owned], bg_s.at[d - 1], bg_r.at[jnp.minimum(z, 4)], at(turn(z, d, 16), y, core, cell))
        for d in far]

    def added(own, slots):
        values = [own] + [slots[d] for d in range(15)]
        while len(values) > 1:
            values = [values[i] + values[i + 1] for i in range(0, len(values), 2)]
        return values[0]

    @pl.when(z < 5)
    def _():
        for d in range(15):
            remote(part_gram.at[0:8], z_gram.at[d], zg_s.at[0], zg_r.at[d], other).wait_recv()
        all_gram[owned] = added(part_gram[owned], z_gram)
        for copy in back_g:
            copy.start()

    arrive(z_c)
    all_cross[mine] = added(part_cross[mine], z_cross)
    back_c = [
        go(all_cross.at[mine], all_cross.at[mine], bc_s.at[d - 1], bc_r.at[d - 1], at(turn(z, d, 16), y, core, cell))
        for d in far]

    for v in range(5):
        pl.when(z != v)(remote(part_gram.at[0:8], all_gram.at[8 * v:8 * v + 8], zg_s.at[0], bg_r.at[v], other).wait_recv)
    rows = tile(core * 160 + y * 40, 40)
    wide_g = [
        go(all_gram, whole_gram.at[cell, rows], yx_s.at[n], yx_r.at[n], at(z, turn(y, dy, 4), core, turn(cell, dx, 4)))
        for n, (dy, dx) in enumerate(plane)]
    whole_gram[cell, rows] = all_gram[...]
    arrive(back_c)
    spot = tile(y * 128, 128)
    side = lanes(core * 128, 128)
    wide_c = [
        go(all_cross, whole_cross.at[spot, side], yc_s.at[d - 1], yc_r.at[d - 1], at(z, turn(y, d, 4), core, cell))
        for d in steps]
    whole_cross[spot, side] = all_cross[...]
    arrive(wide_g)
    half = tile(core * 160, 160)
    pair_g = go(whole_gram.at[:, half], whole_gram.at[:, half], core_s.at[2], core_r.at[2], other)
    arrive(wide_c)
    pair_c = go(whole_cross.at[:, side], whole_cross.at[:, side], core_s.at[3], core_r.at[3], other)
    pair_g.wait_recv()

    place_gram(whole_gram, a_ref)
    d_ref[...] = a_ref[0, :, 0:128]
    lane = lax.broadcasted_iota(jnp.int32, (8, 128), 1)
    sub = lax.broadcasted_iota(jnp.int32, (8, 128), 0)
    cells = whole_cross.shape[1]
    end = 512 + cells

    def block(b, unused):
        held = [d_ref[8 * i:8 * i + 8, :] for i in range(16)]
        for p in range(16):
            held = sweep_rows(held, p, lane, sub)
        for i in range(16):
            d_ref[8 * i:8 * i + 8, :] = -held[i]
        for s in range(4):
            @pl.when(b == s)
            def _():
                if s == 0:
                    pair_c.wait_recv()
                    for i in range(4):
                        a_ref[i, :, 512:end] = whole_cross[128 * i:128 * i + 128]
                begin = 128 * s + 128
                w = jnp.dot(d_ref[...], a_ref[s, :, begin:end], precision=HI, preferred_element_type=F32)
                for i in range(s + 1, 4):
                    here = slice(128 * i, end)
                    a_ref[i, :, here] -= lax.dot_general(
                        a_ref[s, :, 128 * i:128 * i + 128], w[:, 128 * i - begin:], (((0,), (0,)), ((), ())), precision=HI, preferred_element_type=F32)
                a_ref[s, :, begin:end] = w
                if s < 3:
                    d_ref[...] = a_ref[s + 1, :, begin:begin + 128]
        return unused

    lax.fori_loop(0, 4, block, 0)
    column = cell * cells + core * 128
    found = [None] * 4
    handed = []
    for b in (3, 2, 1, 0):
        x = a_ref[b, :, 512:end]
        if b < 3:
            below = jnp.concatenate(found[b + 1:], axis=0)
            x = x - jnp.dot(a_ref[b, :, 128 * b + 128:512], below, precision=HI, preferred_element_type=F32)
        found[b] = x
        x_ref[b] = x
        copy = remote(
            x_ref.at[b, :, side], coef_out.at[:, lanes(column, 128)], x_s.at[b], x_r.at[cell], at(z, y, core, b))
        handed.append((b, copy))
        pl.when(cell != b)(copy.start)

    sums = []
    for b in range(4):
        sq = found[b] * found[b]
        if b == 0:
            sq = jnp.where(lax.broadcasted_iota(jnp.int32, sq.shape, 0) == 0, 0.0, sq)
        sums.append(jnp.sum(sq[0:64], axis=0, keepdims=True))
        sums.append(jnp.sum(sq[64:128], axis=0, keepdims=True))
    total = sums[0]
    for s in sums[1:]:
        total = total + s
    for g in range(GROUPS):
        part = jnp.zeros_like(total)
        for b in range(8):
            part = part + jnp.where(group_ref[b] == g, sums[b], 0.0)
        share_out[g:g + 1] = part / total
    coef_out[:, lanes(cell * cells, cells)] = x_ref[cell]

    passed = []
    for d in (1, 3, 2):
        source = turn(cell, d, 4)
        piece = coef_out.at[:, lanes(source * cells + core * 128, 128)]
        remote(x_ref.at[0, :, side], piece, x_s.at[0], x_r.at[source], other).wait_recv()
        passed.append(go(piece, piece, f_s.at[d - 1], f_r.at[d - 1], other))
    arrive(passed)
    for copy in sent:
        copy.wait_send()
    for v in range(5):
        pl.when(z != v)(to_owner[v].wait_send)
    for b, copy in handed:
        pl.when(cell != b)(copy.wait_send)

    @pl.when(z < 5)
    def _():
        for copy in back_g:
            copy.wait_send()


def fit(points, yields, term_index, block_group):
    hbm = pl.BlockSpec(memory_space=pltpu.HBM)
    vmem = pl.BlockSpec(memory_space=pltpu.VMEM)
    params, samples = points.shape
    cells = yields.shape[1]
    dma = pltpu.SemaphoreType.DMA

    def f32(*shape):
        return pltpu.VMEM(shape, F32)

    return pl.pallas_call(
        fit_kernel,
        out_shape=(jax.ShapeDtypeStruct((TERMS // 4, cells * 4), F32), jax.ShapeDtypeStruct((GROUPS, cells), F32)),
        in_specs=[hbm] * 4,
        out_specs=(vmem, vmem),
        scratch_shapes=[
            f32(params, samples), pltpu.VMEM((samples, cells), BF16), pltpu.VMEM((2, TERMS), jnp.int32), pltpu.SMEM((8,), jnp.int32),
            pltpu.VMEM((TERMS, samples), BF16), f32(TERMS, cells), f32(320, 128),
            f32(160, 128), f32(512, 128), f32(160, 128), f32(512, 128), f32(3, 40, 128), f32(3, 128, 128), f32(40, 128), f32(128, 128),
            f32(15, 8, 128), f32(15, 8, 128), f32(40, 128), f32(128, 128), f32(4, 320, 128), f32(TERMS, cells),
            f32(4, 128, 512 + cells), f32(128, 128), f32(4, 128, cells),
            dma((4,)), dma((4,)), dma((4,)), dma((6,)), dma((6,)), dma((5,)), dma((15,)), dma((15,)), dma((15,)), dma((15,)), dma((5,)),
            dma((15,)), dma((15,)), dma((15,)), dma((15,)), dma((3,)), dma((3,)), dma((4,)), dma((4,)), dma((3,)), dma((3,)),
        ],
        compiler_params=pltpu.CompilerParams(collective_id=0, has_side_effects=True, vmem_limit_bytes=63 << 20),
        name="fit",
    )(points, yields, term_index.T, block_group)


def on_device(points, yields, term_index, block_group):
    coef, sobol = fit(points, yields, term_index, block_group)
    total_samples = points.shape[1] * lax.axis_size("samp")
    return (coef * jnp.sqrt(jnp.float32(total_samples)), sobol)


def solution(mesh):
    placed = (P(None, "samp"), P("samp", "cell"), P(), P())
    return jax.shard_map(
        on_device,
        mesh=mesh,
        in_specs=placed,
        out_specs=(P("cell", None), P(None, "cell")),
        check_vma=False,
    )
```

time: 543 us -> 76.5 us (0.14)
  waiting for transfers between devices: 355 us -> 0 us
  other arithmetic: 127 us -> 1.89 us
  Pallas kernels: 0 us -> 73.2 us
  local copies, waits for them, and re-layouts: 22.3 us -> 0.6 us
  between operations: 16.9 us -> 0.65 us
  matrix products: 14.7 us -> 0 us
    psum x1 -> x0, waiting for transfers between devices: 349 us -> none  [on_device(): gram, cross = lax.psum((gram_local, cross_local), 'samp')]
    another operation x20 -> x0, other arithmetic: 121 us -> none  [the longest x15 79.5 us: on_device(): lower = jnp.linalg.cholesky(gram)]
    pallas_call x0 -> x1, Pallas kernels: none -> 73.2 us  [fit(): pl.pallas_call(fit_kernel, out_shape=(jax.ShapeDtypeStruct((TERMS // 4, c...]
    another operation x19 -> x0, local copies, waits for them, and re-layouts: 11.5 us -> none
    another operation x20 -> x0, matrix products: 9.92 us -> none  [the longest x7 5.79 us: on_device(): lax.linalg.triangular_solve(lower, cross, left_side=True, lower=True)]
    gather x2 -> x0, local copies, waits for them, and re-layouts: 7.18 us -> none  [the longest x1 3.62 us: design(): left = jnp.take(table, term_index[:, 0], axis=0)]
    all_to_all x1 -> x0, waiting for transfers between devices: 5.8 us -> none  [on_device(): lax.all_to_all(scaled, 'cell', split_axis=0, concat_axis=1, tiled=True)]
  transfers between devices with their start and end apart: 2 -> 0, of which waited for: 2 -> 0; matrix products, arithmetic and copies ran while one was open for 0% -> 0% of each run, Pallas kernels for 0% -> 0%
where the time goes in v3:
time: 76.5 us; the launch traced here: 76.3 us
  Pallas kernels  73.2 us (96%)
  other arithmetic  1.89 us (2%)
    pallas_call x1, Pallas kernels, fit(): pl.pallas_call(fit_kernel, out_shape=(jax.ShapeDtypeStruct((TERMS // 4, c...  73.2 us
    mul x1, other arithmetic, on_device(): return (coef * jnp.sqrt(jnp.float32(total_samples)), sobol)  1.89 us

profile of v3, /device:TPU:1, one launch (start us, length us, event | category | flops | bytes accessed | tf_op | source)
XLA Modules:
  0.0 76.3 jit_solution(6215571029791839213)
XLA Ops:
  0.6 73.2 %fit.1 = (f32[128,1024]{1,0:T(8,128)}, f32[8,256]{1,0:T(8,128)}) custom-call(f32[24,2048]{1,0:T(8,128)} %points_hbm.1, bf16[2048,256]{1,0:T(8,128)(2,1)} %yields_hbm.1, s32[2,512]{1,0:T(2,128)} %bitcast.1, s32[8]{0:T(128)} %group_hbm.1), custom_call_target="tpu_custom_call" | custom-call | tf_op jit(solution)/shard_map/fit/pallas_call | solution.py:354
  73.8 0.0 copy-start
  73.8 1.9 %broadcast_multiply_fusion = f32[128,1024]{1,0:T(8,128)} fusion(f32[128,1024]{1,0:T(8,128)} %get-tuple-element.4), kind=kLoop, calls=%fused_computation | loop fusion | flops 131072 | bytes 1048576 | tf_op jit(solution)/shard_map/mul | solution.py:376
  75.7 0.0 copy-done
  75.7 0.6 copy.7
Async XLA Ops:
  73.8 1.9 %copy-start = (f32[8,256]{1,0:T(8,128)S(1)}, f32[8,256]{1,0:T(8,128)}, u32[]{:S(2)}) copy-start(f32[8,256]{1,0:T(8,128)} %get-tuple-element.9) | copy-start | bytes 24580

commit v4 on v3

--- a/solution.py
+++ b/solution.py
@@ -1,3 +1,5 @@
+import functools
+
 import jax
 import jax.numpy as jnp
 from jax import lax
@@ -7,7 +9,6 @@
 
 GROUPS = 8
 TERMS = 512
-HI = lax.Precision.HIGHEST
 MESH = pl.DeviceIdType.MESH
 F32 = jnp.float32
 BF16 = jnp.bfloat16
@@ -25,13 +26,15 @@
     params, samples = points_ref.shape
     width = 3 * params
     place = lax.broadcasted_iota(jnp.int32, (256, TERMS), 0)
+    order = [128 * quarter + 32 * block for block in range(4) for quarter in range(4)]
 
     def pick(column):
         degree = column & 3
         target = (degree - 1) * params + (column >> 2)
         hit = (place == target) | (place == target + width) | (place == target + 2 * width)
         chosen = jnp.where(degree == 0, (place == 3 * width).astype(F32), hit.astype(F32))
-        return chosen.T.astype(BF16)
+        straight = chosen.T
+        return jnp.concatenate([straight[start:start + 32] for start in order], axis=0).astype(BF16)
 
     pick_a = pick(terms_ref[0:1, :])
     pick_b = pick(terms_ref[1:2, :])
@@ -71,19 +74,55 @@
     return jnp.broadcast_to(row, (8, 128))
 
 
-def sweep_rows(rows, p, lane, sub):
+def tree(terms):
+    terms = list(terms)
+    while len(terms) > 1:
+        terms = [terms[i] + terms[i + 1] for i in range(0, len(terms), 2)]
+    return terms[0]
+
+
+def parts(v):
+    a = v.astype(BF16)
+    rest = v - a.astype(F32)
+    b = rest.astype(BF16)
+    return a, b, (rest - b.astype(F32)).astype(BF16)
+
+
+def as_left(v, axis):
+    a, b, c = parts(v)
+    return jnp.concatenate([a, a, b, b, a, c], axis=axis)
+
+
+def as_right(v):
+    a, b, c = parts(v)
+    return jnp.concatenate([a, b, a, b, c, a], axis=0)
+
+
+def mul(left, right, axis):
+    return lax.dot_general(left, right, (((axis,), (0,)), ((), ())), preferred_element_type=F32)
+
+
+def sweep_rows(rows, p, lane, sub, spill):
     pivot = rows[p]
     at = 8 * p
     inside = (lane >= at) & (lane < at + 8)
-    spread = [full(pivot[:, at + j:at + j + 1]) for j in range(8)]
+    target = jnp.where(inside, jnp.where(lane - at == sub, 1.0, 0.0), -pivot)
+    base = 9 * (p % 2)
+    for j in range(8):
+        spill[base + j] = full(pivot[:, at + j:at + j + 1])
+    spill[base + 8] = target
+
+    def row(k, i):
+        return spill[base + k, pl.ds(i, 8, stride=0), :]
+
     m = [[None] * 8 for _ in range(8)]
     for j in range(8):
         for i in range(j + 1):
-            m[i][j] = full(spread[j][i:i + 1, :])
+            m[i][j] = row(j, i)
     for k in range(8):
         r = 1.0 / m[k][k]
-        t = [None if j == k else m[min(j, k)][max(j, k)] * r for j in range(8)]
         old = [m[min(j, k)][max(j, k)] for j in range(8)]
+        t = [None if j == k else old[j] * r for j in range(8)]
         for j in range(8):
             for i in range(j + 1):
                 if i != k and j != k:
@@ -92,23 +131,66 @@
             if j != k:
                 m[min(j, k)][max(j, k)] = t[j]
         m[k][k] = -r
-    target = jnp.where(inside, jnp.where(lane - at == sub, 1.0, 0.0), -pivot)
-    source = [full(target[i:i + 1, :]) for i in range(8)]
-    wide = []
-    for j in range(8):
-        terms = [m[min(i, j)][max(i, j)] * source[i] for i in range(8)]
-        wide.append(((terms[0] + terms[1]) + (terms[2] + terms[3])) + ((terms[4] + terms[5]) + (terms[6] + terms[7])))
-    out = [None] * 16
-    order = [(p + 1 + q) % 16 for q in range(15)]
-    for q in order:
-        terms = [full(rows[q][:, at + j:at + j + 1]) * wide[j] for j in range(8)]
-        total = ((terms[0] + terms[1]) + (terms[2] + terms[3])) + ((terms[4] + terms[5]) + (terms[6] + terms[7]))
-        out[q] = jnp.where(inside, 0.0, rows[q]) - total
+    source = [row(8, i) for i in range(8)]
+    wide = [tree([m[min(i, j)][max(i, j)] * source[i] for i in range(8)]) for j in range(8)]
+    out = list(rows)
+    near = [q for q in (p + 1, p + 2) if q < 16]
+    for q in near:
+        out[q] = jnp.where(inside, 0.0, rows[q]) - tree([full(rows[q][:, at + j:at + j + 1]) * wide[j] for j in range(8)])
     packed = wide[7]
     for j in range(7):
         packed = jnp.where(sub == j, wide[j], packed)
+    u = [v.astype(F32) for v in parts(pivot)]
+    w = [v.astype(F32) for v in parts(packed)]
+    left = jnp.concatenate([u[0], u[0], u[1], u[1], u[0], u[2]], axis=0).astype(BF16)
+    right = jnp.concatenate([w[0], w[1], w[0], w[1], w[2], w[0]], axis=0).astype(BF16)
+    change = mul(left, right, 0)
+    for q in range(16):
+        if q != p and q not in near:
+            out[q] = jnp.where(inside, 0.0, rows[q]) - change[8 * q:8 * q + 8]
     out[p] = packed
     return out
+
+
+def invert(block, spill):
+    lane = lax.broadcasted_iota(jnp.int32, (8, 128), 1)
+    sub = lax.broadcasted_iota(jnp.int32, (8, 128), 0)
+    rows = [block[8 * i:8 * i + 8] for i in range(16)]
+    for p in range(16):
+        rows = sweep_rows(rows, p, lane, sub, spill)
+    return -jnp.concatenate(rows, axis=0)
+
+
+def eliminate(a_ref, spill, late):
+    end = a_ref.shape[2]
+    diag = a_ref[0, :, 0:128]
+    for b in range(4):
+        inverse = invert(diag, spill)
+        if b == 0:
+            late()
+        p = as_left(inverse, 1)
+        begin = 128 * b + 128
+        if b < 3:
+            s1 = a_ref[b, :, begin:begin + 128]
+            w1 = mul(p, as_right(s1), 1)
+            diag = a_ref[b + 1, :, begin:begin + 128] - mul(as_left(s1, 0), as_right(w1), 0)
+            a_ref[b, :, begin:begin + 128] = w1
+        cut = min(begin + 128, 512)
+        s2 = a_ref[b, :, cut:end]
+        w2 = mul(p, as_right(s2), 1)
+        a_ref[b, :, cut:end] = w2
+        if b < 3:
+            right = as_right(w2)
+            a_ref[b + 1, :, cut:end] -= mul(as_left(s1, 0), right, 0)
+            for i in range(b + 2, 4):
+                left = as_left(s2[:, 128 * i - cut:128 * i - cut + 128], 0)
+                a_ref[i, :, 128 * i:end] -= mul(left, right[:, 128 * i - cut:], 0)
+    for b in (3, 2, 1, 0):
+        x = a_ref[b, :, 512:end]
+        yield b, x
+        right = as_right(x)
+        for i in range(b - 1, -1, -1):
+            a_ref[i, :, 512:end] -= mul(as_left(a_ref[i, :, 128 * b:128 * b + 128], 1), right, 1)
 
 
 def place_gram(gram_ref, a_ref):
@@ -126,7 +208,7 @@
     points_hbm, yields_hbm, terms_hbm, group_hbm, coef_out, share_out,
     points_ref, yields_ref, terms_ref, group_ref, psi_ref, cross_ref, gram_ref,
     got_gram, got_cross, half_gram, half_cross, y_gram, y_cross, part_gram, part_cross, z_gram, z_cross,
-    all_gram, all_cross, whole_gram, whole_cross, a_ref, d_ref, x_ref,
+    all_gram, all_cross, whole_gram, whole_cross, a_ref, spill_ref, x_ref,
     load_sem, core_s, core_r, y_s, y_r, zg_s, zg_r, zc_s, zc_r, bg_s, bg_r, bc_s, bc_r, yx_s, yx_r, yc_s, yc_r, x_s, x_r, f_s, f_r,
 ):
     samp, cell = lax.axis_index("samp"), lax.axis_index("cell")
@@ -217,10 +299,7 @@
         for d in far]
 
     def added(own, slots):
-        values = [own] + [slots[d] for d in range(15)]
-        while len(values) > 1:
-            values = [values[i] + values[i + 1] for i in range(0, len(values), 2)]
-        return values[0]
+        return tree([own] + [slots[d] for d in range(15)])
 
     @pl.when(z < 5)
     def _():
@@ -258,59 +337,38 @@
     pair_g.wait_recv()
 
     place_gram(whole_gram, a_ref)
-    d_ref[...] = a_ref[0, :, 0:128]
-    lane = lax.broadcasted_iota(jnp.int32, (8, 128), 1)
-    sub = lax.broadcasted_iota(jnp.int32, (8, 128), 0)
     cells = whole_cross.shape[1]
-    end = 512 + cells
-
-    def block(b, unused):
-        held = [d_ref[8 * i:8 * i + 8, :] for i in range(16)]
-        for p in range(16):
-            held = sweep_rows(held, p, lane, sub)
-        for i in range(16):
-            d_ref[8 * i:8 * i + 8, :] = -held[i]
-        for s in range(4):
-            @pl.when(b == s)
-            def _():
-                if s == 0:
-                    pair_c.wait_recv()
-                    for i in range(4):
-                        a_ref[i, :, 512:end] = whole_cross[128 * i:128 * i + 128]
-                begin = 128 * s + 128
-                w = jnp.dot(d_ref[...], a_ref[s, :, begin:end], precision=HI, preferred_element_type=F32)
-                for i in range(s + 1, 4):
-                    here = slice(128 * i, end)
-                    a_ref[i, :, here] -= lax.dot_general(
-                        a_ref[s, :, 128 * i:128 * i + 128], w[:, 128 * i - begin:], (((0,), (0,)), ((), ())), precision=HI, preferred_element_type=F32)
-                a_ref[s, :, begin:end] = w
-                if s < 3:
-                    d_ref[...] = a_ref[s + 1, :, begin:begin + 128]
-        return unused
-
-    lax.fori_loop(0, 4, block, 0)
+
+    def late():
+        pair_c.wait_recv()
+        for i in range(4):
+            a_ref[i, :, 512:512 + cells] = whole_cross[128 * i:128 * i + 128]
+
     column = cell * cells + core * 128
+    own = lanes(cell * cells, cells)
     found = [None] * 4
     handed = []
-    for b in (3, 2, 1, 0):
-        x = a_ref[b, :, 512:end]
-        if b < 3:
-            below = jnp.concatenate(found[b + 1:], axis=0)
-            x = x - jnp.dot(a_ref[b, :, 128 * b + 128:512], below, precision=HI, preferred_element_type=F32)
+    for b, x in eliminate(a_ref, spill_ref, late):
         found[b] = x
         x_ref[b] = x
-        copy = remote(
-            x_ref.at[b, :, side], coef_out.at[:, lanes(column, 128)], x_s.at[b], x_r.at[cell], at(z, y, core, b))
-        handed.append((b, copy))
-        pl.when(cell != b)(copy.start)
+        for v in range(4):
+            copy = remote(
+                x_ref.at[b, 32 * v:32 * v + 32, side], coef_out.at[32 * b:32 * b + 32, lanes(column, 128)],
+                x_s.at[4 * b + v], x_r.at[4 * b + cell], at(z, y, core, v))
+            handed.append((v, copy))
+            pl.when(cell != v)(copy.start)
+        coef_out[32 * b:32 * b + 32, own] = x_ref[b, tile(cell * 32, 32), :]
 
     sums = []
-    for b in range(4):
-        sq = found[b] * found[b]
-        if b == 0:
-            sq = jnp.where(lax.broadcasted_iota(jnp.int32, sq.shape, 0) == 0, 0.0, sq)
-        sums.append(jnp.sum(sq[0:64], axis=0, keepdims=True))
-        sums.append(jnp.sum(sq[64:128], axis=0, keepdims=True))
+    for quarter in range(4):
+        for low in (0, 2):
+            value = None
+            for b in (low, low + 1):
+                sq = found[b][32 * quarter:32 * quarter + 32] * found[b][32 * quarter:32 * quarter + 32]
+                if quarter == 0 and b == 0:
+                    sq = jnp.where(lax.broadcasted_iota(jnp.int32, sq.shape, 0) == 0, 0.0, sq)
+                value = sq if value is None else value + sq
+            sums.append(jnp.sum(value, axis=0, keepdims=True))
     total = sums[0]
     for s in sums[1:]:
         total = total + s
@@ -319,21 +377,24 @@
         for b in range(8):
             part = part + jnp.where(group_ref[b] == g, sums[b], 0.0)
         share_out[g:g + 1] = part / total
-    coef_out[:, lanes(cell * cells, cells)] = x_ref[cell]
 
     passed = []
-    for d in (1, 3, 2):
-        source = turn(cell, d, 4)
-        piece = coef_out.at[:, lanes(source * cells + core * 128, 128)]
-        remote(x_ref.at[0, :, side], piece, x_s.at[0], x_r.at[source], other).wait_recv()
-        passed.append(go(piece, piece, f_s.at[d - 1], f_r.at[d - 1], other))
+    for n, blocks in enumerate(((3, 2, 1), (0,))):
+        piece_rows = slice(32 * min(blocks), 32 * max(blocks) + 32)
+        for d in (1, 3, 2):
+            source = turn(cell, d, 4)
+            place = lanes(source * cells + core * 128, 128)
+            for b in blocks:
+                remote(x_ref.at[0, 0:32, side], coef_out.at[32 * b:32 * b + 32, place], x_s.at[0], x_r.at[4 * b + source], other).wait_recv()
+            piece = coef_out.at[piece_rows, place]
+            passed.append(go(piece, piece, f_s.at[3 * n + d - 1], f_r.at[3 * n + d - 1], other))
     arrive(passed)
     for copy in sent:
         copy.wait_send()
     for v in range(5):
         pl.when(z != v)(to_owner[v].wait_send)
-    for b, copy in handed:
-        pl.when(cell != b)(copy.wait_send)
+    for v, copy in handed:
+        pl.when(cell != v)(copy.wait_send)
 
     @pl.when(z < 5)
     def _():
@@ -351,6 +412,8 @@
     def f32(*shape):
         return pltpu.VMEM(shape, F32)
 
+    points, yields, terms, block_group = (
+        pltpu.with_memory_space_constraint(v, pltpu.HBM) for v in (points, yields, term_index.T, block_group))
     return pl.pallas_call(
         fit_kernel,
         out_shape=(jax.ShapeDtypeStruct((TERMS // 4, cells * 4), F32), jax.ShapeDtypeStruct((GROUPS, cells), F32)),
@@ -361,19 +424,44 @@
             pltpu.VMEM((TERMS, samples), BF16), f32(TERMS, cells), f32(320, 128),
             f32(160, 128), f32(512, 128), f32(160, 128), f32(512, 128), f32(3, 40, 128), f32(3, 128, 128), f32(40, 128), f32(128, 128),
             f32(15, 8, 128), f32(15, 8, 128), f32(40, 128), f32(128, 128), f32(4, 320, 128), f32(TERMS, cells),
-            f32(4, 128, 512 + cells), f32(128, 128), f32(4, 128, cells),
+            f32(4, 128, 512 + cells), f32(18, 8, 128), f32(4, 128, cells),
             dma((4,)), dma((4,)), dma((4,)), dma((6,)), dma((6,)), dma((5,)), dma((15,)), dma((15,)), dma((15,)), dma((15,)), dma((5,)),
-            dma((15,)), dma((15,)), dma((15,)), dma((15,)), dma((3,)), dma((3,)), dma((4,)), dma((4,)), dma((3,)), dma((3,)),
+            dma((15,)), dma((15,)), dma((15,)), dma((15,)), dma((3,)), dma((3,)), dma((16,)), dma((16,)), dma((6,)), dma((6,)),
         ],
-        compiler_params=pltpu.CompilerParams(collective_id=0, has_side_effects=True, vmem_limit_bytes=63 << 20),
+        compiler_params=pltpu.CompilerParams(collective_id=0, has_side_effects=True, vmem_limit_bytes=48 << 20),
         name="fit",
-    )(points, yields, term_index.T, block_group)
+    )(points, yields, terms, block_group)
+
+
+def finish_kernel(scale, coef_ref, share_ref, coef_hbm, share_hbm, scaled_ref, sem):
+    copies = [pltpu.make_async_copy(share_ref, share_hbm, sem.at[4])]
+    copies[0].start()
+    for n in range(4):
+        rows = slice(32 * n, 32 * n + 32)
+        scaled_ref[rows] = coef_ref[rows] * scale
+        copies.append(pltpu.make_async_copy(scaled_ref.at[rows], coef_hbm.at[rows], sem.at[n]))
+        copies[-1].start()
+    for copy in copies:
+        copy.wait()
+
+
+def finish(coef, share, scale):
+    hbm = pl.BlockSpec(memory_space=pltpu.HBM)
+    vmem = pl.BlockSpec(memory_space=pltpu.VMEM)
+    return pl.pallas_call(
+        functools.partial(finish_kernel, scale),
+        out_shape=(jax.ShapeDtypeStruct(coef.shape, F32), jax.ShapeDtypeStruct(share.shape, F32)),
+        in_specs=[vmem, vmem],
+        out_specs=(hbm, hbm),
+        scratch_shapes=[pltpu.VMEM(coef.shape, F32), pltpu.SemaphoreType.DMA((5,))],
+        compiler_params=pltpu.CompilerParams(vmem_limit_bytes=4 << 20),
+        name="finish",
+    )(coef, share)
 
 
 def on_device(points, yields, term_index, block_group):
     coef, sobol = fit(points, yields, term_index, block_group)
-    total_samples = points.shape[1] * lax.axis_size("samp")
-    return (coef * jnp.sqrt(jnp.float32(total_samples)), sobol)
+    return finish(coef, sobol, float(points.shape[1] * lax.axis_size("samp")) ** 0.5)
 
 
 def solution(mesh):

time: 76.5 us -> 68.7 us (0.90)
  Pallas kernels: 73.2 us -> 67.7 us
  other arithmetic: 1.89 us -> 0 us
    pallas_call x1, Pallas kernels: 73.2 us -> 66.9 us  [fit(): pl.pallas_call(fit_kernel, out_shape=(jax.ShapeDtypeStruct((TERMS // 4, c...]
    mul x1 -> x0, other arithmetic: 1.89 us -> none  [on_device(): return (coef * jnp.sqrt(jnp.float32(total_samples)), sobol)]
    pallas_call x0 -> x1, Pallas kernels: none -> 0.84 us  [finish(): pl.pallas_call(functools.partial(finish_kernel, scale), out_shape=(jax.Sh...]
where the time goes in v4:
time: 68.7 us; the launch traced here: 68.5 us
  Pallas kernels  67.7 us (99%)
  between operations  0.8 us (1%)
    pallas_call x1, Pallas kernels, fit(): pl.pallas_call(fit_kernel, out_shape=(jax.ShapeDtypeStruct((TERMS // 4, c...  66.9 us

profile of v4, /device:TPU:1, one launch (start us, length us, event | category | flops | bytes accessed | tf_op | source)
XLA Modules:
  0.0 68.5 jit_solution(999150640501171341)
XLA Ops:
  0.6 66.9 %fit.1 = (f32[128,1024]{1,0:T(8,128)S(1)}, f32[8,256]{1,0:T(8,128)S(1)}) custom-call(f32[24,2048]{1,0:T(8,128)} %points_hbm.1, bf16[2048,256]{1,0:T(8,128)(2,1)} %yields_hbm.1, s32[2,512]{1,0:T(2,128)} %bitcast.1, s32[8]{0:T(128)} %group_hbm.1), custom_call_target="tpu_custom_call" | custom-call | tf_op jit(solution)/shard_map/fit/pallas_call | solution.py:417
  67.5 0.8 %finish.1 = (f32[128,1024]{1,0:T(8,128)}, f32[8,256]{1,0:T(8,128)}) custom-call(f32[128,1024]{1,0:T(8,128)S(1)} %get-tuple-element.4.coef_ref, f32[8,256]{1,0:T(8,128)S(1)} %get-tuple-element.5.share_ref), custom_call_target="tpu_custom_call" | custom-call | tf_op jit(solution)/shard_map/finish/pallas_call | solution.py:451

commit v5 on v4

--- a/solution.py
+++ b/solution.py
@@ -57,7 +57,9 @@
         psi_ref[:, start:start + step] = (left * right).astype(BF16)
 
 
-def gram_quarter(cell, psi_ref, gram_ref):
+def gram_quarter(cell, psi_ref, gram_ref, corner_ref):
+    corner_ref[...] = lax.dot_general(
+        psi_ref[pl.ds(pl.multiple_of(cell * 32, 32), 32), :], psi_ref[0:128, :], (((1,), (1,)), ((), ())), preferred_element_type=F32)
     low_half = cell < 2
     spots = (
         (0, 128, cell * 128, cell * 128),
@@ -152,39 +154,52 @@
     return out
 
 
-def invert(block, spill):
+def invert(block, spill, between):
     lane = lax.broadcasted_iota(jnp.int32, (8, 128), 1)
     sub = lax.broadcasted_iota(jnp.int32, (8, 128), 0)
     rows = [block[8 * i:8 * i + 8] for i in range(16)]
     for p in range(16):
+        if p in between:
+            between[p]()
         rows = sweep_rows(rows, p, lane, sub, spill)
     return -jnp.concatenate(rows, axis=0)
 
 
-def eliminate(a_ref, spill, late):
+def eliminate(corner, a_ref, spill, between, after):
     end = a_ref.shape[2]
-    diag = a_ref[0, :, 0:128]
+    diag = corner
+    kept = []
+
+    def forward(b):
+        right = as_right(a_ref[b, :, 512:end])
+        for i in range(b + 1, 4):
+            a_ref[i, :, 512:end] -= mul(as_left(a_ref[b, :, 128 * i:128 * i + 128], 0), right, 0)
+        a_ref[b, :, 512:end] = mul(kept[b], right, 1)
+
     for b in range(4):
-        inverse = invert(diag, spill)
-        if b == 0:
-            late()
+        inverse = invert(diag, spill, between.get(b, {}))
+        after.get(b, lambda: None)()
         p = as_left(inverse, 1)
+        kept.append(p)
         begin = 128 * b + 128
         if b < 3:
             s1 = a_ref[b, :, begin:begin + 128]
             w1 = mul(p, as_right(s1), 1)
             diag = a_ref[b + 1, :, begin:begin + 128] - mul(as_left(s1, 0), as_right(w1), 0)
             a_ref[b, :, begin:begin + 128] = w1
-        cut = min(begin + 128, 512)
-        s2 = a_ref[b, :, cut:end]
-        w2 = mul(p, as_right(s2), 1)
-        a_ref[b, :, cut:end] = w2
-        if b < 3:
+        if b < 2:
+            cut = begin + 128
+            s2 = a_ref[b, :, cut:512]
+            w2 = mul(p, as_right(s2), 1)
+            a_ref[b, :, cut:512] = w2
             right = as_right(w2)
-            a_ref[b + 1, :, cut:end] -= mul(as_left(s1, 0), right, 0)
+            a_ref[b + 1, :, cut:512] -= mul(as_left(s1, 0), right, 0)
             for i in range(b + 2, 4):
                 left = as_left(s2[:, 128 * i - cut:128 * i - cut + 128], 0)
-                a_ref[i, :, 128 * i:end] -= mul(left, right[:, 128 * i - cut:], 0)
+                a_ref[i, :, 128 * i:512] -= mul(left, right[:, 128 * i - cut:], 0)
+        if b > 0:
+            forward(b - 1)
+    forward(3)
     for b in (3, 2, 1, 0):
         x = a_ref[b, :, 512:end]
         yield b, x
@@ -194,7 +209,7 @@
 
 
 def place_gram(gram_ref, a_ref):
-    for b in range(4):
+    for b in range(1, 4):
         a_ref[b, :, 128 * b:128 * b + 128] = gram_ref[b, 0:128]
     for b in range(3):
         a_ref[b, :, 128 * b + 128:128 * b + 256] = gram_ref[b, 128:256]
@@ -206,10 +221,10 @@
 
 def fit_kernel(
     points_hbm, yields_hbm, terms_hbm, group_hbm, coef_out, share_out,
-    points_ref, yields_ref, terms_ref, group_ref, psi_ref, cross_ref, gram_ref,
-    got_gram, got_cross, half_gram, half_cross, y_gram, y_cross, part_gram, part_cross, z_gram, z_cross,
+    points_ref, yields_ref, terms_ref, group_ref, psi_ref, cross_ref, gram_ref, corner_ref, near_ref, line_ref, first_ref,
+    y_gram, y_cross, part_gram, part_cross, z_gram, z_cross,
     all_gram, all_cross, whole_gram, whole_cross, a_ref, spill_ref, x_ref,
-    load_sem, core_s, core_r, y_s, y_r, zg_s, zg_r, zc_s, zc_r, bg_s, bg_r, bc_s, bc_r, yx_s, yx_r, yc_s, yc_r, x_s, x_r, f_s, f_r,
+    load_sem, core_s, core_r, y_s, y_r, zg_s, zg_r, zc_s, zc_r, bg_s, bg_r, bc_s, bc_r, yx_s, yx_r, yc_s, yc_r, x_s, x_r, f_s, f_r, n_s, n_r, l_s, l_r, p_s, p_r,
 ):
     samp, cell = lax.axis_index("samp"), lax.axis_index("cell")
     core = lax.rem(samp, 2)
@@ -225,10 +240,11 @@
     other = at(z, y, 1 - core, cell)
     far = (8, 7, 9, 6, 10, 5, 11, 4, 12, 3, 13, 2, 14, 1, 15)
     plane = [(dy, dx) for dy in (2, 1, 3, 0) for dx in (2, 1, 3, 0) if (dy, dx) != (0, 0)]
+    close = (4, 3, 13, 2, 14, 1, 15)
     barrier = pltpu.get_barrier_semaphore()
     greet = [at(turn(z, d, 16), y, core, cell) for d in far]
     greet += [at(z, turn(y, dy, 4), core, turn(cell, dx, 4)) for dy, dx in plane]
-    greet += [other]
+    greet += [other] + [at(z, turn(y, d, 4), 1 - core, cell) for d in (2, 1, 3)]
     for device in greet:
         pl.semaphore_signal(barrier, inc=1, device_id=device, device_id_type=MESH)
 
@@ -243,7 +259,7 @@
     loads[0].wait()
     loads[1].wait()
     basis(terms_ref, points_ref, psi_ref)
-    gram_quarter(cell, psi_ref, gram_ref)
+    gram_quarter(cell, psi_ref, gram_ref, corner_ref)
     loads[2].wait()
     cross_ref[...] = jnp.dot(psi_ref[...], yields_ref[...], preferred_element_type=F32)
     loads[3].wait()
@@ -265,90 +281,109 @@
         for copy in copies:
             copy.wait_recv()
 
-    core_g = go(gram_ref.at[tile((1 - core) * 160, 160)], got_gram, core_s.at[0], core_r.at[0], other)
-    core_c = go(cross_ref.at[:, lanes((1 - core) * 128, 128)], got_cross, core_s.at[1], core_r.at[1], other)
-    core_g.wait_recv()
-    half_gram[...] = gram_ref[tile(core * 160, 160)] + got_gram[...]
-    steps = (2, 1, 3)
+    me = y * 2 + core
+    mates = [
+        (turn(y, dy, 4), 1 - core if flip else core)
+        for dy, flip in ((2, 0), (2, 1), (1, 0), (1, 1), (3, 0), (3, 1), (0, 1))]
+    near_ref[me] = corner_ref[tile(y * 8, 8)]
+    near = [
+        go(corner_ref.at[tile(yy * 8, 8)], near_ref.at[me], n_s.at[n], n_r.at[n], at(z, yy, cc, cell)) for n, (yy, cc) in enumerate(mates)]
     along_g = [
-        go(half_gram.at[tile(turn(y, d, 4) * 40, 40)], y_gram.at[d - 1], y_s.at[d - 1], y_r.at[d - 1], at(z, turn(y, d, 4), core, cell))
-        for d in steps]
-    core_c.wait_recv()
-    half_cross[...] = cross_ref[:, lanes(core * 128, 128)] + got_cross[...]
+        go(gram_ref.at[tile(cc * 160 + yy * 40, 40)], y_gram.at[me], y_s.at[n], y_r.at[n], at(z, yy, cc, cell))
+        for n, (yy, cc) in enumerate(mates)]
     along_c = [
-        go(half_cross.at[tile(turn(y, d, 4) * 128, 128)], y_cross.at[d - 1], y_s.at[d + 2], y_r.at[d + 2], at(z, turn(y, d, 4), core, cell))
-        for d in steps]
-
+        go(cross_ref.at[tile(yy * 128, 128), lanes(cc * 128, 128)], y_cross.at[me], y_s.at[7 + n], y_r.at[7 + n], at(z, yy, cc, cell))
+        for n, (yy, cc) in enumerate(mates)]
+    y_gram[me] = gram_ref[tile(core * 160 + y * 40, 40)]
+    y_cross[me] = cross_ref[tile(y * 128, 128), lanes(core * 128, 128)]
+    arrive(near)
+    line_ref[z] = tree([near_ref[n] for n in range(8)])
+    line = [go(line_ref.at[z], line_ref.at[z], l_s.at[d - 1], l_r.at[d - 1], at(turn(z, d, 16), y, core, cell)) for d in far]
+
+    kind = lax.rem(z, 8)
     arrive(along_g)
-    part_gram[...] = (half_gram[tile(y * 40, 40)] + y_gram[0]) + (y_gram[1] + y_gram[2])
+    part_gram[...] = tree([y_gram[n] for n in range(8)])
     to_owner = []
     for v in range(5):
-        slot = lax.rem(z + 31 - v, 16)
-        copy = remote(part_gram.at[8 * v:8 * v + 8], z_gram.at[jnp.minimum(slot, 14)], zg_s.at[v], zg_r.at[jnp.minimum(slot, 14)], at(v, y, core, cell))
-        to_owner.append(copy)
-        pl.when(z != v)(copy.start)
+        for half in (0, 1):
+            copy = remote(
+                part_gram.at[8 * v:8 * v + 8], z_gram.at[z], zg_s.at[2 * v + half], zg_r.at[z], at(v + 8 * half, y, core, cell))
+            to_owner.append((v + 8 * half, copy))
+            pl.when(z != v + 8 * half)(copy.start)
     arrive(along_c)
-    part_cross[...] = (half_cross[tile(y * 128, 128)] + y_cross[0]) + (y_cross[1] + y_cross[2])
+    part_cross[...] = tree([y_cross[n] for n in range(8)])
+    mine = tile(kind * 16, 16)
+    z_cross[z] = part_cross[mine]
     z_c = [
-        go(part_cross.at[tile(turn(z, d, 16) * 8, 8)], z_cross.at[d - 1], zc_s.at[d - 1], zc_r.at[d - 1], at(turn(z, d, 16), y, core, cell))
+        go(part_cross.at[tile(lax.rem(z + d, 8) * 16, 16)], z_cross.at[z], zc_s.at[d - 1], zc_r.at[d - 1], at(turn(z, d, 16), y, core, cell))
         for d in far]
-    mine = tile(z * 8, 8)
-    owned = tile(jnp.minimum(z, 4) * 8, 8)
+    owned = tile(jnp.minimum(kind, 4) * 8, 8)
     back_g = [
-        remote(all_gram.at[owned], all_gram.at[owned], bg_s.at[d - 1], bg_r.at[jnp.minimum(z, 4)], at(turn(z, d, 16), y, core, cell))
-        for d in far]
-
-    def added(own, slots):
-        return tree([own] + [slots[d] for d in range(15)])
-
-    @pl.when(z < 5)
+        remote(all_gram.at[owned], all_gram.at[owned], bg_s.at[n], bg_r.at[jnp.minimum(kind, 4)], at(turn(z, d, 16), y, core, cell))
+        for n, d in enumerate(close)]
+
+    arrive(line)
+    corner = tile(cell * 32 + y * 8, 8)
+    first_ref[corner] = tree([line_ref[n] for n in range(16)])
+    first = [
+        go(first_ref.at[corner], first_ref.at[corner], p_s.at[n], p_r.at[n], at(z, turn(y, dy, 4), core, turn(cell, dx, 4)))
+        for n, (dy, dx) in enumerate(plane)]
+
+    @pl.when(kind < 5)
     def _():
-        for d in range(15):
-            remote(part_gram.at[0:8], z_gram.at[d], zg_s.at[0], zg_r.at[d], other).wait_recv()
-        all_gram[owned] = added(part_gram[owned], z_gram)
+        z_gram[z] = part_gram[owned]
+        for d in range(1, 16):
+            source = turn(z, d, 16)
+            remote(part_gram.at[0:8], z_gram.at[source], zg_s.at[0], zg_r.at[source], other).wait_recv()
+        all_gram[owned] = tree([z_gram[n] for n in range(16)])
         for copy in back_g:
             copy.start()
 
     arrive(z_c)
-    all_cross[mine] = added(part_cross[mine], z_cross)
+    all_cross[mine] = tree([z_cross[n] for n in range(16)])
     back_c = [
-        go(all_cross.at[mine], all_cross.at[mine], bc_s.at[d - 1], bc_r.at[d - 1], at(turn(z, d, 16), y, core, cell))
-        for d in far]
-
-    for v in range(5):
-        pl.when(z != v)(remote(part_gram.at[0:8], all_gram.at[8 * v:8 * v + 8], zg_s.at[0], bg_r.at[v], other).wait_recv)
+        go(all_cross.at[mine], all_cross.at[mine], bc_s.at[n], bc_r.at[n], at(turn(z, d, 16), y, core, cell))
+        for n, d in enumerate(close)]
+
     rows = tile(core * 160 + y * 40, 40)
-    wide_g = [
-        go(all_gram, whole_gram.at[cell, rows], yx_s.at[n], yx_r.at[n], at(z, turn(y, dy, 4), core, turn(cell, dx, 4)))
-        for n, (dy, dx) in enumerate(plane)]
-    whole_gram[cell, rows] = all_gram[...]
-    arrive(back_c)
+    half = tile(core * 160, 160)
     spot = tile(y * 128, 128)
     side = lanes(core * 128, 128)
-    wide_c = [
-        go(all_cross, whole_cross.at[spot, side], yc_s.at[d - 1], yc_r.at[d - 1], at(z, turn(y, d, 4), core, cell))
-        for d in steps]
-    whole_cross[spot, side] = all_cross[...]
-    arrive(wide_g)
-    half = tile(core * 160, 160)
-    pair_g = go(whole_gram.at[:, half], whole_gram.at[:, half], core_s.at[2], core_r.at[2], other)
-    arrive(wide_c)
-    pair_c = go(whole_cross.at[:, side], whole_cross.at[:, side], core_s.at[3], core_r.at[3], other)
-    pair_g.wait_recv()
-
-    place_gram(whole_gram, a_ref)
     cells = whole_cross.shape[1]
-
-    def late():
-        pair_c.wait_recv()
+    wide_g, wide_c = [], []
+
+    def spread_gram():
+        for v in range(5):
+            apart = lax.rem(z + 16 - v, 8)
+            pl.when(apart != 0)(remote(part_gram.at[0:8], all_gram.at[8 * v:8 * v + 8], zg_s.at[0], bg_r.at[v], other).wait_recv)
+        for n, (dy, dx) in enumerate(plane):
+            wide_g.append(go(
+                all_gram, whole_gram.at[cell, rows], yx_s.at[n], yx_r.at[n], at(z, turn(y, dy, 4), core, turn(cell, dx, 4))))
+        whole_gram[cell, rows] = all_gram[...]
+
+    def spread_cross():
+        arrive(back_c)
+        for n, (yy, cc) in enumerate(mates):
+            wide_c.append(go(all_cross, whole_cross.at[spot, side], yc_s.at[n], yc_r.at[n], at(z, yy, cc, cell)))
+        whole_cross[spot, side] = all_cross[...]
+
+    def take_gram():
+        arrive(wide_g)
+        pair_g = go(whole_gram.at[:, half], whole_gram.at[:, half], core_s.at[0], core_r.at[0], other)
+        pair_g.wait_recv()
+        place_gram(whole_gram, a_ref)
+
+    def take_cross():
+        arrive(wide_c)
         for i in range(4):
             a_ref[i, :, 512:512 + cells] = whole_cross[128 * i:128 * i + 128]
 
+    arrive(first)
     column = cell * cells + core * 128
     own = lanes(cell * cells, cells)
     found = [None] * 4
     handed = []
-    for b, x in eliminate(a_ref, spill_ref, late):
+    for b, x in eliminate(first_ref[...], a_ref, spill_ref, {0: {2: spread_gram, 11: spread_cross}}, {0: take_gram, 1: take_cross}):
         found[b] = x
         x_ref[b] = x
         for v in range(4):
@@ -378,6 +413,16 @@
             part = part + jnp.where(group_ref[b] == g, sums[b], 0.0)
         share_out[g:g + 1] = part / total
 
+    for copy in sent:
+        copy.wait_send()
+    for v, copy in to_owner:
+        pl.when(z != v)(copy.wait_send)
+
+    @pl.when(kind < 5)
+    def _():
+        for copy in back_g:
+            copy.wait_send()
+
     passed = []
     for n, blocks in enumerate(((3, 2, 1), (0,))):
         piece_rows = slice(32 * min(blocks), 32 * max(blocks) + 32)
@@ -387,19 +432,14 @@
             for b in blocks:
                 remote(x_ref.at[0, 0:32, side], coef_out.at[32 * b:32 * b + 32, place], x_s.at[0], x_r.at[4 * b + source], other).wait_recv()
             piece = coef_out.at[piece_rows, place]
-            passed.append(go(piece, piece, f_s.at[3 * n + d - 1], f_r.at[3 * n + d - 1], other))
+            copy = remote(piece, piece, f_s.at[3 * n + d - 1], f_r.at[3 * n + d - 1], other)
+            copy.start()
+            passed.append(copy)
     arrive(passed)
-    for copy in sent:
+    for copy in passed:
         copy.wait_send()
-    for v in range(5):
-        pl.when(z != v)(to_owner[v].wait_send)
     for v, copy in handed:
         pl.when(cell != v)(copy.wait_send)
-
-    @pl.when(z < 5)
-    def _():
-        for copy in back_g:
-            copy.wait_send()
 
 
 def fit(points, yields, term_index, block_group):
@@ -422,11 +462,13 @@
         scratch_shapes=[
             f32(params, samples), pltpu.VMEM((samples, cells), BF16), pltpu.VMEM((2, TERMS), jnp.int32), pltpu.SMEM((8,), jnp.int32),
             pltpu.VMEM((TERMS, samples), BF16), f32(TERMS, cells), f32(320, 128),
-            f32(160, 128), f32(512, 128), f32(160, 128), f32(512, 128), f32(3, 40, 128), f32(3, 128, 128), f32(40, 128), f32(128, 128),
-            f32(15, 8, 128), f32(15, 8, 128), f32(40, 128), f32(128, 128), f32(4, 320, 128), f32(TERMS, cells),
+            f32(32, 128), f32(8, 8, 128), f32(16, 8, 128), f32(128, 128),
+            f32(8, 40, 128), f32(8, 128, 128), f32(40, 128), f32(128, 128),
+            f32(16, 8, 128), f32(16, 16, 128), f32(40, 128), f32(128, 128), f32(4, 320, 128), f32(TERMS, cells),
             f32(4, 128, 512 + cells), f32(18, 8, 128), f32(4, 128, cells),
-            dma((4,)), dma((4,)), dma((4,)), dma((6,)), dma((6,)), dma((5,)), dma((15,)), dma((15,)), dma((15,)), dma((15,)), dma((5,)),
-            dma((15,)), dma((15,)), dma((15,)), dma((15,)), dma((3,)), dma((3,)), dma((16,)), dma((16,)), dma((6,)), dma((6,)),
+            dma((4,)), dma((1,)), dma((1,)), dma((14,)), dma((14,)), dma((10,)), dma((16,)), dma((15,)), dma((15,)),
+            dma((7,)), dma((5,)), dma((7,)), dma((7,)), dma((15,)), dma((15,)), dma((7,)), dma((7,)),
+            dma((16,)), dma((16,)), dma((6,)), dma((6,)), dma((7,)), dma((7,)), dma((15,)), dma((15,)), dma((15,)), dma((15,)),
         ],
         compiler_params=pltpu.CompilerParams(collective_id=0, has_side_effects=True, vmem_limit_bytes=48 << 20),
         name="fit",

time: 68.7 us -> 67 us (0.975)
  Pallas kernels: 67.7 us -> 66 us
    pallas_call x1, Pallas kernels: 66.9 us -> 65.2 us  [fit(): pl.pallas_call(fit_kernel, out_shape=(jax.ShapeDtypeStruct((TERMS // 4, c...]
where the time goes in v5:
time: 67 us; the launch traced here: 66.8 us
  Pallas kernels  66 us (99%)
  between operations  0.8 us (1%)
    pallas_call x1, Pallas kernels, fit(): pl.pallas_call(fit_kernel, out_shape=(jax.ShapeDtypeStruct((TERMS // 4, c...  65.2 us

profile of v5, /device:TPU:1, one launch (start us, length us, event | category | flops | bytes accessed | tf_op | source)
XLA Modules:
  0.0 66.8 jit_solution(12949617819642402987)
XLA Ops:
  0.6 65.2 %fit.1 = (f32[128,1024]{1,0:T(8,128)S(1)}, f32[8,256]{1,0:T(8,128)S(1)}) custom-call(f32[24,2048]{1,0:T(8,128)} %points_hbm.1, bf16[2048,256]{1,0:T(8,128)(2,1)} %yields_hbm.1, s32[2,512]{1,0:T(2,128)} %bitcast.1, s32[8]{0:T(128)} %group_hbm.1), custom_call_target="tpu_custom_call" | custom-call | tf_op jit(solution)/shard_map/fit/pallas_call | solution.py:457
  65.8 0.8 %finish.1 = (f32[128,1024]{1,0:T(8,128)}, f32[8,256]{1,0:T(8,128)}) custom-call(f32[128,1024]{1,0:T(8,128)S(1)} %get-tuple-element.4.coef_ref, f32[8,256]{1,0:T(8,128)S(1)} %get-tuple-element.5.share_ref), custom_call_target="tpu_custom_call" | custom-call | tf_op jit(solution)/shard_map/finish/pallas_call | solution.py:493

commit v6 on v5

--- a/solution.py
+++ b/solution.py
@@ -176,29 +176,35 @@
             a_ref[i, :, 512:end] -= mul(as_left(a_ref[b, :, 128 * i:128 * i + 128], 0), right, 0)
         a_ref[b, :, 512:end] = mul(kept[b], right, 1)
 
+    def trail(b, s1):
+        cut = 128 * b + 256
+        s2 = a_ref[b, :, cut:512]
+        w2 = mul(kept[b], as_right(s2), 1)
+        a_ref[b, :, cut:512] = w2
+        right = as_right(w2)
+        a_ref[b + 1, :, cut:512] -= mul(as_left(s1, 0), right, 0)
+        for i in range(b + 2, 4):
+            left = as_left(s2[:, 128 * i - cut:128 * i - cut + 128], 0)
+            a_ref[i, :, 128 * i:512] -= mul(left, right[:, 128 * i - cut:], 0)
+
     for b in range(4):
-        inverse = invert(diag, spill, between.get(b, {}))
+        steps = dict(between.get(b, {}))
+        if b in (1, 2):
+            steps[2] = functools.partial(trail, b - 1, s1)
+        if b == 2:
+            steps[6] = functools.partial(forward, 0)
+        if b == 3:
+            steps[2] = functools.partial(forward, 1)
+            steps[7] = functools.partial(forward, 2)
+        inverse = invert(diag, spill, steps)
         after.get(b, lambda: None)()
-        p = as_left(inverse, 1)
-        kept.append(p)
+        kept.append(as_left(inverse, 1))
         begin = 128 * b + 128
         if b < 3:
             s1 = a_ref[b, :, begin:begin + 128]
-            w1 = mul(p, as_right(s1), 1)
+            w1 = mul(kept[b], as_right(s1), 1)
             diag = a_ref[b + 1, :, begin:begin + 128] - mul(as_left(s1, 0), as_right(w1), 0)
             a_ref[b, :, begin:begin + 128] = w1
-        if b < 2:
-            cut = begin + 128
-            s2 = a_ref[b, :, cut:512]
-            w2 = mul(p, as_right(s2), 1)
-            a_ref[b, :, cut:512] = w2
-            right = as_right(w2)
-            a_ref[b + 1, :, cut:512] -= mul(as_left(s1, 0), right, 0)
-            for i in range(b + 2, 4):
-                left = as_left(s2[:, 128 * i - cut:128 * i - cut + 128], 0)
-                a_ref[i, :, 128 * i:512] -= mul(left, right[:, 128 * i - cut:], 0)
-        if b > 0:
-            forward(b - 1)
     forward(3)
     for b in (3, 2, 1, 0):
         x = a_ref[b, :, 512:end]
@@ -378,12 +384,13 @@
         for i in range(4):
             a_ref[i, :, 512:512 + cells] = whole_cross[128 * i:128 * i + 128]
 
+    spread_gram()
     arrive(first)
     column = cell * cells + core * 128
     own = lanes(cell * cells, cells)
     found = [None] * 4
     handed = []
-    for b, x in eliminate(first_ref[...], a_ref, spill_ref, {0: {2: spread_gram, 11: spread_cross}}, {0: take_gram, 1: take_cross}):
+    for b, x in eliminate(first_ref[...], a_ref, spill_ref, {0: {11: spread_cross}, 2: {5: take_cross}}, {0: take_gram}):
         found[b] = x
         x_ref[b] = x
         for v in range(4):

time: 67 us -> 66.5 us (level)
  no operation moved by 1% of the time
where the time goes in v6:
time: 66.5 us; the launch traced here: 66.4 us
  Pallas kernels  65.6 us (99%)
  between operations  0.8 us (1%)
    pallas_call x1, Pallas kernels, fit(): pl.pallas_call(fit_kernel, out_shape=(jax.ShapeDtypeStruct((TERMS // 4, c...  64.8 us

profile of v6, /device:TPU:1, one launch (start us, length us, event | category | flops | bytes accessed | tf_op | source)
XLA Modules:
  0.0 66.4 jit_solution(11350227670582226643)
XLA Ops:
  0.6 64.8 %fit.1 = (f32[128,1024]{1,0:T(8,128)S(1)}, f32[8,256]{1,0:T(8,128)S(1)}) custom-call(f32[24,2048]{1,0:T(8,128)} %points_hbm.1, bf16[2048,256]{1,0:T(8,128)(2,1)} %yields_hbm.1, s32[2,512]{1,0:T(2,128)} %bitcast.1, s32[8]{0:T(128)} %group_hbm.1), custom_call_target="tpu_custom_call" | custom-call | tf_op jit(solution)/shard_map/fit/pallas_call | solution.py:464
  65.4 0.8 %finish.1 = (f32[128,1024]{1,0:T(8,128)}, f32[8,256]{1,0:T(8,128)}) custom-call(f32[128,1024]{1,0:T(8,128)S(1)} %get-tuple-element.4.coef_ref, f32[8,256]{1,0:T(8,128)S(1)} %get-tuple-element.5.share_ref), custom_call_target="tpu_custom_call" | custom-call | tf_op jit(solution)/shard_map/finish/pallas_call | solution.py:500
